TPU v7x, 32 devices: a whole 2x2x4 slice. The times are simulated.
32 devices in a mesh: expert: 16 (over z, y, x), dp: 2 (over core).
Axes of the slice: x: 2, y: 2, z: 4, core: 2. Of those that a mesh axis runs over, the one named last changes fastest.
Arguments:
- pooled: bfloat16 [8192, 256], P(('expert', 'dp')), may hold values from -6 to 6
- routes: int32 [8192, 2], P(('expert', 'dp')), may hold values from 0 to 15, all different within a row; in each aligned block of 256 rows (0 to 255, 256 to 511, ...) at most 48 rows name the same one
- labels: int32 [8192, 2], P(('expert', 'dp')), may hold values from 0 to 1
- in_weight: bfloat16 [16, 4096, 256], P('expert'), may hold values from -0.375 to 0.375
- out_weight: bfloat16 [16, 4096, 256], P('expert'), may hold values from -0.09375 to 0.09375
- gate_weight: bfloat16 [16, 2, 256], replicated, may hold values from -0.375 to 0.375
- tower_weight: float32 [2, 256], replicated, may hold values from -0.375 to 0.375
- tower_bias: float32 [2], replicated, may hold values from -3 to 3
- bag_rows: int32 [16384], P(('expert', 'dp')), may hold values from 0 to 1023
- bag_sample: int32 [16384], P(('expert', 'dp')), may hold values from 0 to 255
- bag_weight: float32 [16384], P(('expert', 'dp')), may hold values from 0.5 to 2
- row_table: float32 [16384, 256], P('expert'), may hold values from -6 to 6
Outputs:
- in_grad: float32 [16, 4096, 256], P('expert', 'dp')
- out_grad: float32 [16, 4096, 256], P('expert', 'dp')
- gate_grad: float32 [16, 2, 256], P('expert')
- tower_grad: float32 [2, 256], replicated
- new_table: float32 [16384, 256], P('expert')
Inputs may be any that keep to these rules, and one draw needn't show every extreme that they name: `routes`: within each device's 256 rows no expert is named more than 48 times, a bound that some block reaches; a row's two experts differ.
All inputs are finite; a program needn't handle non-finite values.
Results may differ from a plain program's by a relative error of at most 0.0041.
Values may be sent and summed in bfloat16 or wider, within the bound.
A program may use at most 128 MiB of HBM per device.

v0:
```python
import functools

import jax
import jax.numpy as jnp
from jax import lax
from jax.experimental import pallas as pl
from jax.experimental.pallas import tpu as pltpu
from jax.sharding import PartitionSpec as P

LOSS_SCALE = 32.0
STEP_SIZE = 0.25
F32, BF16 = jnp.float32, jnp.bfloat16
MESH = pl.DeviceIdType.MESH
VMEM_LIMIT = 62 * 2**20


def mm(left, right, left_dim=1, right_dim=0):
    return lax.dot_general(
        left, right, (((left_dim,), (right_dim,)), ((), ())), preferred_element_type=F32
    )


def nt(left, right):
    return mm(left, right, 1, 1)


def halves(value):
    high = value.astype(BF16).astype(F32)
    return high, value - high


def stacked(value):
    return jnp.concatenate(halves(value), axis=0).astype(BF16)


def folded(value):
    return value[:8] + value[8:]


def sigmoid(value):
    return 0.5 * jnp.tanh(0.5 * value) + 0.5


def iota(shape, dim):
    return lax.broadcasted_iota(jnp.int32, shape, dim)


def one_hot(condition):
    return jnp.where(condition, 1.0, 0.0)


def exchange(count, me, source, target, send_sem, recv_sem):
    def copy(peer, slot):
        return pltpu.make_async_remote_copy(
            src_ref=source.at[peer],
            dst_ref=target.at[slot],
            send_sem=send_sem.at[peer],
            recv_sem=recv_sem.at[slot],
            device_id={"expert": peer},
            device_id_type=MESH,
        )

    def start():
        @pl.loop(1, count)
        def _(step):
            copy(lax.rem(me + step, count), me).start()

        target[me] = source[me]

    def wait():
        @pl.loop(1, count)
        def _(step):
            peer = lax.rem(me + step, count)
            copy(peer, peer).wait_recv()

    def drain():
        @pl.loop(1, count)
        def _(step):
            copy(lax.rem(me + step, count), me).wait_send()

    return start, wait, drain


def kernel(
    sizes,
    pooled_ref,
    routes_rows_ref,
    labels_ref,
    in_hbm,
    out_hbm,
    gate_ref,
    tower_ref,
    bias_ref,
    bag_rows_ref,
    bag_sample_ref,
    bag_weight_ref,
    in_mine_hbm,
    in_recv_hbm,
    hidden_parts_ref,
    small_ref,
    grads_ref,
    rows_ref,
    in_ref,
    out_ref,
    turned_ref,
    proj_rows_ref,
    proj_cols_ref,
    act_ref,
    slope_ref,
    pre_ref,
    place_ref,
    a_send,
    a_recv,
    b_send,
    b_recv,
    c_send,
    c_recv,
    d_send,
    d_recv,
    e_send,
    e_recv,
    r_send,
    r_recv,
    t_send,
    t_recv,
    s_send,
    s_recv,
    in_mine,
    in_other,
    hidden_other,
    rows_acc,
    back_acc,
    send_sem,
    recv_sem,
    dp_send,
    dp_recv,
    local_sem,
):
    count, cap, chunk, chunks, per_owner = sizes
    rows_all = count * cap
    tok_rows = pooled_ref.shape[0]
    me, core = lax.axis_index("expert"), lax.axis_index("dp")
    other = 1 - core
    half = chunks // 2

    def phase(index, source, target):
        return exchange(count, me, source, target, send_sem.at[index], recv_sem.at[index])

    a_start, a_wait, a_drain = phase(0, a_send, a_recv)
    b_start, b_wait, b_drain = phase(1, b_send, b_recv)
    c_start, c_wait, c_drain = phase(2, c_send, c_recv)
    d_start, d_wait, d_drain = phase(3, d_send, d_recv)
    e_start, e_wait, e_drain = phase(4, e_send, e_recv)
    r_start, r_wait, r_drain = phase(5, r_send, r_recv)
    t_start, t_wait, t_drain = phase(6, t_send, t_recv)

    def to_other(index, source, target):
        return pltpu.make_async_remote_copy(
            src_ref=source,
            dst_ref=target,
            send_sem=dp_send.at[index],
            recv_sem=dp_recv.at[index],
            device_id={"dp": other},
            device_id_type=MESH,
        )

    barrier = pltpu.get_barrier_semaphore()

    @pl.loop(1, count)
    def _(step):
        pl.semaphore_signal(
            barrier, inc=1, device_id={"expert": lax.rem(me + step, count)}, device_id_type=MESH
        )

    pl.semaphore_signal(barrier, inc=1, device_id={"dp": other}, device_id_type=MESH)
    load_out = pltpu.make_async_copy(out_hbm, out_ref, local_sem.at[0])
    load_in = pltpu.make_async_copy(in_hbm, in_ref, local_sem.at[1])
    load_out.start()
    load_in.start()

    first_row, second_row = routes_rows_ref[0:1, :], routes_rows_ref[1:2, :]
    first_map = one_hot(iota((count, tok_rows), 0) == first_row)
    second_map = one_hot(iota((count, tok_rows), 0) == second_row)
    above = one_hot(
        iota((tok_rows, tok_rows), 0) < iota((tok_rows, tok_rows), 1)
    ).astype(BF16)
    first_total = jnp.sum(first_map, axis=1, keepdims=True)
    first_rank = jnp.sum(first_map * mm(first_map.astype(BF16), above), axis=0, keepdims=True)
    second_rank = jnp.sum(
        second_map * (mm(second_map.astype(BF16), above) + first_total), axis=0, keepdims=True
    )
    first_slot = first_rank.astype(jnp.int32) + first_row * cap
    second_slot = second_rank.astype(jnp.int32) + second_row * cap
    places = iota((rows_all, tok_rows), 0)
    fill = one_hot((places == first_slot) | (places == second_slot)).astype(BF16)
    place_ref[...] = fill
    a_send[...] = mm(fill, pooled_ref[...]).astype(BF16).reshape(a_send.shape)

    @pl.loop(0, count)
    def _(owner):
        line = bag_rows_ref[pl.ds(owner * per_owner // 128, 1), :]
        shift = lax.rem(128 - lax.rem(owner * per_owner, 128), 128)
        line = pltpu.roll(jnp.broadcast_to(line, (8, 128)), shift, 1)
        r_send[owner] = jnp.where(iota((8, 128), 1) < per_owner, line, -1)

    pl.semaphore_wait(barrier, count)
    a_start()
    r_start()

    lanes = iota((128, tok_rows), 0)
    first_at = one_hot(lanes == first_rank.astype(jnp.int32)).astype(BF16)
    second_at = one_hot(lanes == second_rank.astype(jnp.int32)).astype(BF16)
    signed = first_map - second_map
    row_of = iota((8, tok_rows), 0)
    labels = jnp.where(row_of == 0, labels_ref[0:1, :], labels_ref[1:2, :]).astype(F32)
    bias = jnp.where(row_of == 0, bias_ref[0], bias_ref[1])
    gates = [gate_ref[:, task, :] for task in range(2)]
    feat_row = iota((8, tower_ref.shape[1]), 0)
    tower_rows = jnp.where(
        feat_row == 0, tower_ref[0:1, :], jnp.where(feat_row == 1, tower_ref[1:2, :], 0.0)
    )
    sample_wide = jnp.broadcast_to(bag_sample_ref[...].astype(F32), (8, bag_sample_ref.shape[1]))
    weight_wide = jnp.broadcast_to(bag_weight_ref[...], (8, bag_sample_ref.shape[1]))
    sample_col, weight_col = sample_wide.T[:, 0:1], weight_wide.T[:, 0:1]
    bag = one_hot(
        iota((bag_sample_ref.shape[1], tok_rows), 1) == sample_col.astype(jnp.int32)
    ).astype(BF16)
    gate_logit = jnp.zeros((8, tok_rows), F32)
    for task in range(2):
        logits = nt(gates[task], pooled_ref[...])
        gate_logit = jnp.where(
            row_of == task, jnp.sum(signed * logits, axis=0, keepdims=True), gate_logit
        )
    gate_first = sigmoid(gate_logit)
    gate_second = 1.0 - gate_first
    tower_high, tower_low = halves(tower_rows)
    tower_high, tower_low = tower_high.astype(BF16), tower_low.astype(BF16)
    load_out.wait()
    load_in.wait()

    @pl.loop(0, chunks)
    def _(step):
        span = pl.ds(pl.multiple_of(step * chunk, chunk), chunk)
        weights = out_ref[span, :]
        proj_rows_ref[step] = stacked(nt(tower_high, weights) + nt(tower_low, weights))
        proj_cols_ref[span, :] = nt(weights, tower_high) + nt(weights, tower_low)
        turned_ref[step] = in_ref[span, :].T

    a_wait()
    rows_acc[...] = jnp.zeros_like(rows_acc)

    @pl.loop(0, chunks)
    def _(step):
        span = pl.ds(pl.multiple_of(step * chunk, chunk), chunk)
        before = nt(in_ref[span, :], a_recv[...].reshape(rows_all, -1))
        near = 0.5 * before
        bend = jnp.tanh(near)
        bent = near * bend
        slope_ref[span, :] = (1.0 + bend) + (near - bent * bend)
        act = (near + bent).astype(BF16)
        act_ref[span, :] = act
        rows_acc[...] += mm(proj_rows_ref[step], act)

    dots = folded(rows_acc[...])

    @pl.loop(0, count)
    def _(peer):
        b_send[peer] = pltpu.roll(dots, lax.rem(rows_all - peer * cap, rows_all), 1)[:, :128]

    b_start()
    b_wait()
    owner_of = iota((count * 8, tok_rows), 0) // 8
    first_mask = one_hot(owner_of == first_row)
    second_mask = one_hot(owner_of == second_row)
    got_high, got_low = halves(
        jnp.where(iota((count * 8, 128), 1) < cap, b_recv[...].reshape(count * 8, 128), 0.0)
    )

    def pick(mask, where):
        found = mm(got_high.astype(BF16), where) + mm(got_low.astype(BF16), where)
        return jnp.sum((mask * found).reshape(count, 8, tok_rows), axis=0)

    first_dot, second_dot = pick(first_mask, first_at), pick(second_mask, second_at)
    task_logit = gate_first * first_dot + gate_second * second_dot + bias
    logit_grad = LOSS_SCALE * (sigmoid(task_logit) - labels)
    first_grad = logit_grad * (first_dot - second_dot) * gate_first * gate_second
    lower = pltpu.roll(first_grad, 2, 0)
    keep = row_of < 4
    first_vals = jnp.where(keep, jnp.where(row_of < 2, gate_first * logit_grad, lower), 0.0)
    second_vals = jnp.where(keep, jnp.where(row_of < 2, gate_second * logit_grad, -lower), 0.0)

    def spread(vals, mask, where):
        wide = jnp.broadcast_to(vals[None], (count, 8, tok_rows)).reshape(count * 8, tok_rows)
        high, low = halves(wide * mask)
        return nt(high.astype(BF16), where) + nt(low.astype(BF16), where)

    c_send[...] = (
        spread(first_vals, first_mask, first_at) + spread(second_vals, second_mask, second_at)
    ).reshape(c_send.shape)
    c_start()
    gate_input = jnp.zeros((tok_rows, pooled_ref.shape[1]), F32)
    for task in range(2):
        high, low = halves(signed * first_grad[task : task + 1, :])
        weights = gates[task]
        gate_input += mm(high.astype(BF16), weights, 0, 0) + mm(low.astype(BF16), weights, 0, 0)
    c_wait()
    coefs = jnp.zeros((8, rows_all), F32)
    blank = jnp.zeros((8, rows_all - 128), F32)

    def place(peer, total):
        return total + pltpu.roll(
            jnp.concatenate([c_recv[peer], blank], axis=1), peer * cap, 1
        )

    coefs = lax.fori_loop(0, count, place, coefs)
    coef_zero, coef_one = 0.5 * coefs[0:1, :], 0.5 * coefs[1:2, :]
    back_acc[...] = jnp.zeros_like(back_acc)

    @pl.loop(0, chunks)
    def _(step):
        span = pl.ds(pl.multiple_of(step * chunk, chunk), chunk)
        cols = proj_cols_ref[span, :]
        hidden_grad = cols[:, 0:1] * coef_zero + cols[:, 1:2] * coef_one
        grad = (hidden_grad * slope_ref[span, :]).astype(BF16)
        pre_ref[span, :] = grad
        back_acc[...] += mm(turned_ref[step], grad)

    d_send[...] = back_acc[...].T.astype(BF16).reshape(d_send.shape)
    d_start()

    coef_rows = stacked(coefs)

    def weight_chunk(step, in_target, hidden_target, slot):
        span = pl.ds(pl.multiple_of(step * chunk, chunk), chunk)
        in_target[pl.ds(pl.multiple_of(slot * chunk, chunk), chunk), :] = mm(
            pre_ref[span, :], a_recv[...].reshape(rows_all, -1)
        )
        hidden = folded(nt(coef_rows, act_ref[span, :]))
        hidden_target[slot] = hidden
        return folded(mm(stacked(hidden), out_ref[span, :]))

    tower = jnp.zeros((8, pooled_ref.shape[1]), F32)
    tower = lax.fori_loop(
        0,
        half,
        lambda i, total: total + weight_chunk(other * half + i, in_other, hidden_other, i),
        tower,
    )
    in_copy = to_other(0, in_other, in_recv_hbm)
    hidden_copy = to_other(1, hidden_other, hidden_parts_ref.at[1])
    in_copy.start()
    hidden_copy.start()
    tower = lax.fori_loop(
        0,
        half,
        lambda i, total: total
        + weight_chunk(core * half + i, in_mine, hidden_parts_ref.at[0], i),
        tower,
    )
    gate = folded(mm(coef_rows, a_recv[...].reshape(rows_all, -1)))
    tile = jnp.where(iota(tower.shape, 0) < 2, tower, gate)
    t_send[...] = jnp.broadcast_to(tile[None], t_send.shape)
    t_start()
    store_in = pltpu.make_async_copy(in_mine, in_mine_hbm, local_sem.at[0])
    store_in.start()
    d_wait()
    pooled_grad = gate_input + mm(
        place_ref[...], d_recv[...].reshape(rows_all, -1), 0, 0
    )
    high, low = halves(pooled_grad)
    bag_grad = mm(bag, high.astype(BF16)) + mm(bag, low.astype(BF16))
    e_send[...] = (weight_col * bag_grad).astype(BF16).reshape(e_send.shape)
    e_start()
    r_wait()
    rows_copy = to_other(3, r_recv, rows_ref.at[core])
    rows_copy.start()
    rows_ref[core] = r_recv[...]
    t_wait()
    summed = lax.fori_loop(0, count, lambda i, total: total + t_recv[i], jnp.zeros_like(tower))
    mine = jnp.where(iota(tower.shape, 0) < 2, summed, tile)
    s_send[...] = mine
    small_copy = to_other(4, s_send, s_recv)
    small_copy.start()
    e_wait()
    grads_copy = to_other(2, e_recv, grads_ref.at[core])
    grads_copy.start()
    grads_ref[core] = e_recv[...]
    small_copy.wait()
    small_ref[...] = mine + s_recv[...]
    store_in.wait()
    for copy in (in_copy, hidden_copy, rows_copy, grads_copy):
        copy.wait()
    for drain in (a_drain, b_drain, c_drain, d_drain, e_drain, r_drain, t_drain):
        drain()


def on_device(
    pooled,
    routes,
    labels,
    in_weight,
    out_weight,
    gate_weight,
    tower_weight,
    tower_bias,
    bag_rows,
    bag_sample,
    bag_weight,
    row_table,
):
    count = lax.axis_size("expert")
    tok_rows, feature = pooled.shape
    tasks = tower_weight.shape[0]
    hidden = in_weight.shape[1]
    cap = -(-(3 * tok_rows // count) // 8) * 8
    rows_all = count * cap
    chunk = 1024 if rows_all * 1024 < 2**20 else 512
    chunks = hidden // chunk
    per_owner = bag_rows.shape[0] // count
    held = -(-per_owner // 8) * 8

    def bags(values, empty):
        if held == per_owner:
            return values
        return jnp.pad(
            values.reshape(count, per_owner), ((0, 0), (0, held - per_owner)), constant_values=empty
        )

    vmem = pl.BlockSpec(memory_space=pltpu.VMEM)
    anywhere = pl.BlockSpec(memory_space=pl.ANY)
    scalars = (count, 8, 128)
    routed = (count, cap, feature)
    owned = (count, held, feature)
    half_rows = hidden // 2
    in_mine, in_other, hidden_parts, small, grads, rows = pl.pallas_call(
        functools.partial(kernel, (count, cap, chunk, chunks, per_owner)),
        out_shape=(
            jax.ShapeDtypeStruct((half_rows, feature), F32),
            jax.ShapeDtypeStruct((half_rows, feature), F32),
            jax.ShapeDtypeStruct((2, chunks // 2, 8, chunk), F32),
            jax.ShapeDtypeStruct((8, feature), F32),
            jax.ShapeDtypeStruct((2,) + owned, BF16),
            jax.ShapeDtypeStruct((2,) + scalars, jnp.int32),
        ),
        in_specs=[vmem] * 3
        + [anywhere] * 2
        + [vmem] * 2
        + [pl.BlockSpec(memory_space=pltpu.SMEM)]
        + [vmem] * 3,
        out_specs=(anywhere,) * 2 + (vmem,) * 4,
        scratch_shapes=[
            pltpu.VMEM((hidden, feature), BF16),
            pltpu.VMEM((hidden, feature), BF16),
            pltpu.VMEM((chunks, feature, chunk), BF16),
            pltpu.VMEM((chunks, 16, chunk), BF16),
            pltpu.VMEM((hidden, 8), F32),
            pltpu.VMEM((hidden, rows_all), BF16),
            pltpu.VMEM((hidden, rows_all), F32),
            pltpu.VMEM((hidden, rows_all), BF16),
            pltpu.VMEM((rows_all, tok_rows), BF16),
            pltpu.VMEM(routed, BF16),
            pltpu.VMEM(routed, BF16),
            pltpu.VMEM(scalars, F32),
            pltpu.VMEM(scalars, F32),
            pltpu.VMEM(scalars, F32),
            pltpu.VMEM(scalars, F32),
            pltpu.VMEM(routed, BF16),
            pltpu.VMEM(routed, BF16),
            pltpu.VMEM(owned, BF16),
            pltpu.VMEM(owned, BF16),
            pltpu.VMEM(scalars, jnp.int32),
            pltpu.VMEM(scalars, jnp.int32),
            pltpu.VMEM((count, 8, feature), F32),
            pltpu.VMEM((count, 8, feature), F32),
            pltpu.VMEM((8, feature), F32),
            pltpu.VMEM((8, feature), F32),
            pltpu.VMEM((half_rows, feature), F32),
            pltpu.VMEM((half_rows, feature), F32),
            pltpu.VMEM((chunks // 2, 8, chunk), F32),
            pltpu.VMEM((16, rows_all), F32),
            pltpu.VMEM((feature, rows_all), F32),
            pltpu.SemaphoreType.DMA((7, count)),
            pltpu.SemaphoreType.DMA((7, count)),
            pltpu.SemaphoreType.DMA((5,)),
            pltpu.SemaphoreType.DMA((5,)),
            pltpu.SemaphoreType.DMA((2,)),
        ],
        compiler_params=pltpu.CompilerParams(
            collective_id=0, has_side_effects=True, vmem_limit_bytes=VMEM_LIMIT
        ),
    )(
        pooled,
        routes.T,
        labels.T,
        in_weight[0],
        out_weight[0],
        gate_weight,
        tower_weight,
        tower_bias,
        bag_rows.reshape(-1, 128),
        bags(bag_sample, -1).reshape(1, -1),
        bags(bag_weight, 0.0).reshape(1, -1),
    )
    in_grad = (in_mine + in_other)[None]
    hidden_sum = (hidden_parts[0] + hidden_parts[1])[:, :tasks, :]
    out_grad = sum(
        hidden_sum[:, t].reshape(-1, 1) * tower_weight[t][None, :] for t in range(tasks)
    )[None]
    owned_rows = rows[:, :, 0, :held].reshape(-1)
    matches = (
        jnp.arange(row_table.shape[0], dtype=jnp.int32)[:, None] == owned_rows[None, :]
    ).astype(BF16)
    new_table = row_table - STEP_SIZE * mm(matches, grads.reshape(-1, feature))
    return (in_grad, out_grad, small[None, tasks : 2 * tasks], small[:tasks], new_table)


def solution(mesh):
    in_specs = (
        P(("expert", "dp"), None),
        P(("expert", "dp"), None),
        P(("expert", "dp"), None),
        P("expert", None, None),
        P("expert", None, None),
        P(),
        P(),
        P(),
        P(("expert", "dp")),
        P(("expert", "dp")),
        P(("expert", "dp")),
        P("expert", None),
    )
    out_specs = (
        P("expert", "dp", None),
        P("expert", "dp", None),
        P("expert", None, None),
        P(),
        P("expert", None),
    )
    return jax.shard_map(
        on_device, mesh=mesh, in_specs=in_specs, out_specs=out_specs, check_vma=False
    )
```

profile of v0, /device:TPU:0, one launch (start us, length us, event | category | flops | bytes accessed | tf_op | source)
XLA Modules:
  0.0 75.9 jit_solution(3881921973833604883)
XLA Ops:
  0.6 66.2 %shard_map.155 = (f32[2048,256]{1,0:T(8,128)}, f32[2048,256]{1,0:T(8,128)}, f32[2,2,8,1024]{3,2,1,0:T(8,128)}, f32[8,256]{1,0:T(8,128)}, bf16[2,16,32,256]{3,2,1,0:T(8,128)(2,1)}, /*index=5*/s32[2,16,8,128]{3,2,1,0:T(8,128)}) custom-call(bf16[256,256]{1,0:T(8,128)(2,1)} %pooled_ref.1, s32[2,256]{1,0:T(2,128)} %bitcast.25, s32[2,256]{1,0:T(2,128)} %bitcast.26, ...), custom_call_target="tpu_custom_call" | custom-call | tf_op jit(solution)/shard_map/pallas_call | solution.py:435
  66.9 0.0 copy-start.1
  66.9 0.0 copy-start
  66.9 3.8 %add_bitcast_fusion = f32[1,2048,256]{2,1,0:T(8,128)} fusion(f32[2048,256]{1,0:T(8,128)} %get-tuple-element.11, f32[2048,256]{1,0:T(8,128)} %get-tuple-element.12), kind=kLoop, calls=%fused_computation.4 | loop fusion | flops 524288 | bytes 6291456 | tf_op jit(solution)/shard_map/broadcast_in_dim | solution.py:504
  70.7 0.0 copy-done.1
  70.7 0.0 copy-start.2
  70.7 0.0 copy-start.3
  70.7 0.0 copy-start.4
  70.8 0.0 copy-done
  70.8 1.7 %multiply_add_fusion = f32[1,2048,256]{2,1,0:T(8,128)} fusion(f32[256]{0:T(256)S(1)} %bitcast.24, f32[2048]{0:T(1024)S(1)} %bitcast.22, f32[256]{0:T(256)S(1)} %bitcast.23, f32[2048]{0:T(1024)S(1)} %bitcast.21), kind=kLoop, calls=%fused_computation.3 | loop fusion | flops 1572864 | bytes 2115584 | tf_op jit(solution)/shard_map/add | solution.py:506
  72.5 0.0 copy-done.2
  72.5 0.6 fusion.5
  73.1 0.9 %slice_reduce_fusion = s32[2,16,32]{2,1,0:T(8,128)S(1)} fusion(s32[2,16,8,128]{3,2,1,0:T(8,128)} %get-tuple-element.15), kind=kLoop, calls=%fused_computation.8 | loop fusion | bytes 8192 | tf_op jit(solution)/shard_map/slice | solution.py:509
  74.0 0.1 eq.16
  74.1 0.0 copy-done.3
  74.1 0.0 copy-done.4
  74.1 1.8 %fusion.3 = f32[1024,256]{1,0:T(8,128)} fusion(f32[1024,256]{1,0:T(8,128)S(1)} %copy-done.3, bf16[1024,256]{1,0:T(8,128)(2,1)S(1)} %bitcast.30, s32[1024]{0:T(1024)S(1)} %eq.16), kind=kOutput, calls=%fused_computation.6 | convolution fusion | flops 538443776 | bytes 2625536 | tf_op jit(solution)/shard_map/dot_general | solution.py:18
  (3 shorter events, 0.0 us)
Async XLA Ops:
  66.9 3.9 %copy-start.1 = (f32[2,256]{1,0:T(2,128)S(1)}, f32[2,256]{1,0:T(2,128)}, u32[]{:S(2)}) copy-start(f32[2,256]{1,0:T(2,128)} %tower_ref.1) | copy-start | bytes 6148
  66.9 3.9 %copy-start = (f32[2,2,8,1024]{3,2,1,0:T(8,128)S(1)}, f32[2,2,8,1024]{3,2,1,0:T(8,128)}, u32[]{:S(2)}) copy-start(f32[2,2,8,1024]{3,2,1,0:T(8,128)} %get-tuple-element.13) | copy-start | bytes 393220
  70.7 1.7 %copy-start.2 = (f32[8,256]{1,0:T(8,128)S(1)}, f32[8,256]{1,0:T(8,128)}, u32[]{:S(2)}) copy-start(f32[8,256]{1,0:T(8,128)} %get-tuple-element.14) | copy-start | bytes 24580
  70.7 3.4 %copy-start.3 = (f32[1024,256]{1,0:T(8,128)S(1)}, f32[1024,256]{1,0:T(8,128)}, u32[]{:S(2)}) copy-start(f32[1024,256]{1,0:T(8,128)} %param.23) | copy-start | bytes 3145732
  70.7 3.4 %copy-start.4 = (bf16[2,16,32,256]{3,2,1,0:T(8,128)(2,1)S(1)}, bf16[2,16,32,256]{3,2,1,0:T(8,128)(2,1)}, u32[]{:S(2)}) copy-start(bf16[2,16,32,256]{3,2,1,0:T(8,128)(2,1)} %get-tuple-element.16) | copy-start | bytes 1572868
where the time goes:
time: 76.1 us; the launch traced here: 75.9 us
  Pallas kernels  66.2 us (87%)
  other arithmetic  5.53 us (7%)
  matrix products  1.81 us (2%)
  local copies, waits for them, and re-layouts  1.64 us (2%)
    pallas_call x1, Pallas kernels, on_device(): pl.pallas_call(functools.partial(kernel, (count, cap, chunk, chunks, per_...  66.2 us
    broadcast_in_dim x1, other arithmetic, on_device(): in_grad = (in_mine + in_other)[None]  3.85 us
    dot_general x1, matrix products, mm(): lax.dot_general(left, right, (((left_dim,), (right_dim,)), ((), ())), pre...  1.81 us
    add x1, other arithmetic, on_device(): sum((hidden_sum[:, t].reshape(-1, 1) * tower_weight[t][None, :] for t in...  1.68 us

commit v1 on v0

v1 whole, which is shorter than its diff:
```python
import functools

import jax
import jax.numpy as jnp
from jax import lax
from jax.experimental import pallas as pl
from jax.experimental.pallas import tpu as pltpu
from jax.sharding import PartitionSpec as P

LOSS_SCALE = 32.0
STEP_SIZE = 0.25
F32, BF16 = jnp.float32, jnp.bfloat16
MESH = pl.DeviceIdType.MESH
VMEM_LIMIT = 56 * 2**20
SLOT_BASE = 4096


def mm(left, right, left_dim=1, right_dim=0):
    return lax.dot_general(
        left, right, (((left_dim,), (right_dim,)), ((), ())), preferred_element_type=F32
    )


def nt(left, right):
    return mm(left, right, 1, 1)


def halves(value):
    high = value.astype(BF16).astype(F32)
    return high, value - high


def stacked(value):
    return jnp.concatenate(halves(value), axis=0).astype(BF16)


def folded(value):
    half = value.shape[0] // 2
    return value[:half] + value[half:]


def sigmoid(value):
    return 0.5 * jnp.tanh(0.5 * value) + 0.5


def iota(shape, dim):
    return lax.broadcasted_iota(jnp.int32, shape, dim)


def one_hot(condition):
    return jnp.where(condition, 1.0, 0.0)


def lane_pack(pieces, width, lanes):
    lane = iota(pieces[0].shape, 1)
    rolled = [pltpu.roll(p, i * width % 128, 1) if i * width % 128 else p for i, p in enumerate(pieces)]
    parts = []
    for start in range(0, lanes, 128):
        total = jnp.zeros_like(pieces[0])
        for i, piece in enumerate(rolled):
            low, high = i * width - start, (i + 1) * width - start
            if high > 0 and low < 128:
                total = jnp.where((lane >= low) & (lane < high), piece, total)
        parts.append(total)
    return jnp.concatenate(parts, axis=1)


def kernel(
    sizes,
    pooled_hbm,
    routes_hbm,
    labels_hbm,
    in_hbm,
    out_hbm,
    gate_hbm,
    tower_hbm,
    bias_hbm,
    bag_rows_hbm,
    bag_sample_hbm,
    bag_weight_hbm,
    table_hbm,
    in_sum_ref,
    out_sum_ref,
    gate_sum_ref,
    tower_sum_ref,
    table_ref,
    pooled_ref,
    routes_rows_ref,
    labels_ref,
    gate_ref,
    tower_ref,
    bias_ref,
    bag_rows_ref,
    bag_sample_ref,
    bag_weight_ref,
    in_ref,
    out_ref,
    turned_ref,
    proj_rows_ref,
    proj_cols_ref,
    act_ref,
    slope_ref,
    pre_ref,
    bag_place_ref,
    bag_acc,
    bag_weights,
    a_send,
    a_recv,
    m_send,
    m_recv,
    b_send,
    b_recv,
    d_send,
    d_recv,
    e_send,
    e_recv,
    e_other,
    t_send,
    t_recv,
    s_send,
    s_recv,
    rows_mine,
    rows_other,
    hidden_mine,
    hidden_other,
    hidden_recv,
    rows_acc,
    back_acc,
    send_sem,
    recv_sem,
    dp_send,
    dp_recv,
    local_sem,
):
    count, cap, chunk, chunks, per_owner = sizes
    rows_all = count * cap
    tok_rows, feature = pooled_hbm.shape
    me, core = lax.axis_index("expert"), lax.axis_index("dp")
    other = 1 - core
    half = chunks // 2
    group = count // 2
    slots = group * cap
    blocks = slots // 128
    near = lax.div(me, group)
    far = 1 - near
    place_in = lax.rem(me, group)
    held = e_send.shape[1]
    entries = count * held

    def remote(phase, peer, source, target):
        return pltpu.make_async_remote_copy(
            src_ref=source,
            dst_ref=target,
            send_sem=send_sem.at[phase, peer],
            recv_sem=recv_sem.at[phase, me],
            device_id={"expert": peer},
            device_id_type=MESH,
        )

    def arrival(phase, peer, source, target):
        return pltpu.make_async_remote_copy(
            src_ref=source,
            dst_ref=target,
            send_sem=send_sem.at[phase, peer],
            recv_sem=recv_sem.at[phase, peer],
            device_id={"expert": peer},
            device_id_type=MESH,
        )

    def peers(which, act):
        if which == "far":

            @pl.loop(0, group)
            def _(step):
                act(far * group + lax.rem(place_in + step, group))

        else:

            @pl.loop(1, group)
            def _(step):
                act(near * group + lax.rem(place_in + step, group))

    def everyone(act):
        peers("far", act)
        peers("near", act)

    def to_other(index, source, target):
        return pltpu.make_async_remote_copy(
            src_ref=source,
            dst_ref=target,
            send_sem=dp_send.at[index],
            recv_sem=dp_recv.at[index],
            device_id={"dp": other},
            device_id_type=MESH,
        )

    def a_copy(make, peer):
        return make(0, peer, a_send.at[peer], a_recv.at[me if make is remote else peer])

    def m_copy(make, peer):
        return make(1, peer, m_send.at[peer], m_recv.at[me if make is remote else peer])

    def b_copy(make, peer, index):
        return make(2 + index, peer, b_send.at[index], b_recv.at[me if make is remote else peer, index])

    def d_copy(make, peer):
        return make(4, peer, d_send.at[peer], d_recv.at[me if make is remote else peer])

    def e_copy(make, peer):
        return make(5, peer, e_send.at[peer], e_recv.at[me if make is remote else peer])

    def t_copy(make, peer):
        return make(6, peer, t_send, t_recv.at[me if make is remote else peer])

    barrier = pltpu.get_barrier_semaphore()

    @pl.loop(1, count)
    def _(step):
        pl.semaphore_signal(
            barrier, inc=1, device_id={"expert": lax.rem(me + step, count)}, device_id_type=MESH
        )

    pl.semaphore_signal(barrier, inc=1, device_id={"dp": other}, device_id_type=MESH)
    loads = [
        pltpu.make_async_copy(source, target, local_sem.at[index])
        for index, (source, target) in enumerate(
            (
                (routes_hbm, routes_rows_ref),
                (pooled_hbm, pooled_ref),
                (labels_hbm, labels_ref),
                (bag_rows_hbm, bag_rows_ref),
                (tower_hbm, tower_ref),
                (out_hbm, out_ref),
                (in_hbm, in_ref),
                (gate_hbm, gate_ref),
                (bias_hbm, bias_ref),
                (bag_sample_hbm, bag_sample_ref),
                (bag_weight_hbm, bag_weight_ref),
                (table_hbm, table_ref),
            )
        )
    ]
    for load in loads:
        load.start()
    loads[0].wait()

    first_row, second_row = routes_rows_ref[0:1, :], routes_rows_ref[1:2, :]
    first_map = one_hot(iota((count, tok_rows), 0) == first_row)
    second_map = one_hot(iota((count, tok_rows), 0) == second_row)
    above = one_hot(
        iota((tok_rows, tok_rows), 0) < iota((tok_rows, tok_rows), 1)
    ).astype(BF16)
    before = mm(jnp.concatenate([first_map, second_map], axis=0).astype(BF16), above)
    first_total = jnp.sum(first_map, axis=1, keepdims=True)
    first_rank = jnp.sum(first_map * before[:count], axis=0, keepdims=True).astype(jnp.int32)
    second_rank = jnp.sum(
        second_map * (before[count:] + first_total), axis=0, keepdims=True
    ).astype(jnp.int32)
    first_slot = first_rank + first_row * cap
    second_slot = second_rank + second_row * cap

    def fill_of(index):
        places = iota((slots, tok_rows), 0) + index * slots
        return one_hot((places == first_slot) | (places == second_slot)).astype(BF16)

    def send_half(index):
        rows = 0.5 * mm(fill_of(index), pooled_ref[...])
        a_send[pl.ds(index * group, group)] = rows.astype(BF16).reshape(group, cap, feature)

    loads[1].wait()
    send_half(near)
    pl.semaphore_wait(barrier, count)
    peers("near", lambda peer: a_copy(remote, peer).start())
    send_half(far)
    peers("far", lambda peer: a_copy(remote, peer).start())
    a_recv[me] = a_send[me]
    for load in loads[2:5]:
        load.wait()

    lanes = iota((128, tok_rows), 0)
    first_at = one_hot(lanes == first_rank).astype(BF16)
    second_at = one_hot(lanes == second_rank).astype(BF16)
    label_code = 2 * labels_ref[0:1, :] + labels_ref[1:2, :] + 1

    def partner(own_map, row, rank):
        code = (4 * rank + label_code).astype(F32)
        return jnp.concatenate([own_map * row.astype(F32), own_map * code], axis=0).astype(BF16)

    told = nt(partner(first_map, second_row, second_rank), first_at) + nt(
        partner(second_map, first_row, first_rank), second_at
    )
    code = told[count:]
    meta = jnp.where(
        code > 0.0, SLOT_BASE * told[:count] + code + (4 * cap * place_in).astype(F32), 0.0
    )
    piece_lane = iota((1, 128), 1)
    for owner in range(count):
        start = owner * per_owner
        line = bag_rows_ref[start // 128 : start // 128 + 1, :].astype(F32)
        if start % 128:
            line = pltpu.roll(jnp.broadcast_to(line, (8, 128)), 128 - start % 128, 1)[0:1, :]
        m_send[owner, 0:1, :] = meta[owner : owner + 1, :]
        m_send[owner, 1:2, :] = jnp.where(piece_lane < per_owner, line, -1.0)
    everyone(lambda peer: m_copy(remote, peer).start())
    m_recv[me] = m_send[me]

    feat_row = iota((8, feature), 0)
    tower_rows = jnp.where(
        feat_row == 0, tower_ref[0:1, :], jnp.where(feat_row == 1, tower_ref[1:2, :], 0.0)
    )
    tower_high, tower_low = halves(tower_rows)
    tower_high, tower_low = tower_high.astype(BF16), tower_low.astype(BF16)
    for load in loads[5:11]:
        load.wait()

    @pl.loop(0, chunks)
    def _(step):
        span = pl.ds(pl.multiple_of(step * chunk, chunk), chunk)
        weights = out_ref[span, :]
        proj_rows_ref[step] = stacked(nt(tower_high, weights) + nt(tower_low, weights))
        cols = nt(weights, tower_high) + nt(weights, tower_low)
        proj_cols_ref[0, span, :] = jnp.broadcast_to(cols[:, 0:1], (chunk, 128))
        proj_cols_ref[1, span, :] = jnp.broadcast_to(cols[:, 1:2], (chunk, 128))
        turned_ref[step] = in_ref[span, :].T

    rows_acc[...] = jnp.zeros_like(rows_acc)
    back_acc[...] = jnp.zeros_like(back_acc)

    def forward(index):
        lane_span = pl.ds(pl.multiple_of(index * slots, 128), slots)
        features = a_recv.at[pl.ds(index * group, group)]

        @pl.loop(0, chunks)
        def _(step):
            span = pl.ds(pl.multiple_of(step * chunk, chunk), chunk)
            close = nt(in_ref[span, :], features[...].reshape(slots, feature))
            bend = jnp.tanh(close)
            bent = close * bend
            slope_ref[span, lane_span] = (1.0 + bend) + (close - bent * bend)
            act = (close + bent).astype(BF16)
            act_ref[span, lane_span] = act
            rows_acc[:, lane_span] += mm(proj_rows_ref[step], act)

        dots = folded(rows_acc[:, lane_span])
        tile_row = iota((8, 128), 0)
        tile = jnp.zeros((8, 128), F32)
        for task in range(2):
            for block in range(blocks):
                piece = dots[task : task + 1, block * 128 : (block + 1) * 128]
                tile = jnp.where(tile_row == task * blocks + block, piece, tile)
        b_send[index] = tile
        b_recv[me, index] = tile
        everyone(lambda peer: b_copy(remote, peer, index).start())

    peers("near", lambda peer: a_copy(arrival, peer).wait_recv())
    forward(near)
    peers("far", lambda peer: a_copy(arrival, peer).wait_recv())
    forward(far)

    everyone(lambda peer: m_copy(arrival, peer).wait_recv())
    pieces = [m_recv[source] for source in range(count)]
    told = jnp.concatenate(
        [lane_pack(pieces[i * group : (i + 1) * group], cap, slots)[0:1, :] for i in range(2)],
        axis=1,
    ).astype(jnp.int32)
    bag_lanes = -(-entries // 128) * 128
    rows_mine[...] = jnp.broadcast_to(
        lane_pack(pieces, held, bag_lanes)[1:2, :entries], rows_mine.shape
    )
    rows_copy = to_other(2, rows_mine, rows_other)
    rows_copy.start()
    valid = told > 0
    pair_expert = lax.shift_right_logical(told, 12)
    pair_code = jnp.bitwise_and(told, SLOT_BASE - 1) - 1
    pair_slot = lax.shift_right_logical(pair_code, 2)
    row_wide = iota((8, rows_all), 0)
    slot_labels = jnp.where(
        row_wide == 0,
        jnp.bitwise_and(lax.shift_right_logical(pair_code, 1), 1),
        jnp.bitwise_and(pair_code, 1),
    ).astype(F32)

    def dot_key(expert, slot):
        lane_of = one_hot(
            iota((128, slot.shape[1]), 0) == jnp.bitwise_and(slot, 127)
        ).astype(BF16)
        return lane_of, expert * 8 + lax.shift_right_logical(slot, 7)

    def look_up(tiles, key):
        lane_of, row_of_key = key
        found = folded(mm(tiles, lane_of))
        rows = iota(found.shape, 0)
        return [
            jnp.sum(
                jnp.where(rows == row_of_key + task * blocks, found, 0.0), axis=0, keepdims=True
            )
            for task in range(2)
        ]

    pair_key = dot_key(pair_expert, pair_slot)
    gates = [gate_ref[:, task, :] for task in range(2)]
    expert_row = iota((count, rows_all), 0)
    sign = one_hot(expert_row == me) - one_hot(expert_row == pair_expert)
    features_all = a_recv[...].reshape(rows_all, feature)
    slot_gate = jnp.zeros((8, rows_all), F32)
    for task in range(2):
        logits = nt(gates[task], features_all)
        slot_gate = jnp.where(
            row_wide == task, jnp.sum(sign * logits, axis=0, keepdims=True), slot_gate
        )
    own_gate = 0.5 * jnp.tanh(slot_gate) + 0.5
    pair_gate = 1.0 - own_gate
    gate_both = own_gate * pair_gate
    slot_bias = jnp.where(row_wide == 0, bias_ref[0], bias_ref[1])

    row_of = iota((8, tok_rows), 0)
    labels = jnp.where(row_of == 0, labels_ref[0:1, :], labels_ref[1:2, :]).astype(F32)
    bias = jnp.where(row_of == 0, bias_ref[0], bias_ref[1])
    signed = first_map - second_map
    gate_logit = jnp.zeros((8, tok_rows), F32)
    for task in range(2):
        logits = nt(gates[task], pooled_ref[...])
        gate_logit = jnp.where(
            row_of == task, jnp.sum(signed * logits, axis=0, keepdims=True), gate_logit
        )
    gate_first = sigmoid(gate_logit)
    gate_second = 1.0 - gate_first
    first_key = dot_key(first_row, first_rank + cap * place_in)
    second_key = dot_key(second_row, second_rank + cap * place_in)
    sample_wide = jnp.broadcast_to(bag_sample_ref[...].astype(F32), (8, entries))
    weight_wide = jnp.broadcast_to(bag_weight_ref[...], (8, entries))
    sample_col, weight_col = sample_wide.T[:, 0:1], weight_wide.T[:, 0:1]
    bag = one_hot(iota((entries, tok_rows), 1) == sample_col.astype(jnp.int32)).astype(BF16)
    for index in range(2):
        bag_place_ref[:, index * slots : (index + 1) * slots] = nt(bag, fill_of(index)).astype(BF16)

    for index in range(2):
        everyone(lambda peer, index=index: b_copy(arrival, peer, index).wait_recv())

    own_dot = folded(rows_acc[...])
    pair_dot = []
    for index in range(2):
        lane_span = slice(index * slots, (index + 1) * slots)
        tiles = stacked(b_recv[:, index].reshape(count * 8, 128))
        found = look_up(tiles, (pair_key[0][:, lane_span], pair_key[1][:, lane_span]))
        pair_dot.append(jnp.where(iota((8, slots), 0) == 0, found[0], found[1]))
    pair_dot = jnp.concatenate(pair_dot, axis=1)
    task_logit = own_gate * own_dot + pair_gate * pair_dot + slot_bias
    logit_grad = jnp.where(valid, LOSS_SCALE * (sigmoid(task_logit) - slot_labels), 0.0)
    gate_grad = pltpu.roll(logit_grad * (own_dot - pair_dot) * gate_both, 2, 0)
    coefs = jnp.where(
        row_wide < 2, own_gate * logit_grad, jnp.where(row_wide < 4, gate_grad, 0.0)
    )
    rows_acc[0:8, :] = coefs

    def backward(index):
        lane_span = pl.ds(pl.multiple_of(index * slots, 128), slots)
        coef_zero, coef_one = rows_acc[0:1, lane_span], rows_acc[1:2, lane_span]

        @pl.loop(0, chunks)
        def _(step):
            span = pl.ds(pl.multiple_of(step * chunk, chunk), chunk)
            zero, one = (
                jnp.concatenate([proj_cols_ref[task, span, :]] * blocks, axis=1) for task in range(2)
            )
            hidden_grad = zero * coef_zero + one * coef_one
            grad = (hidden_grad * slope_ref[span, lane_span]).astype(BF16)
            pre_ref[span, lane_span] = grad
            back_acc[:, lane_span] += mm(turned_ref[step], grad)

        back = 0.5 * back_acc[:, lane_span].T
        d_send[pl.ds(index * group, group)] = back.astype(BF16).reshape(group, cap, feature)

    backward(far)
    peers("far", lambda peer: d_copy(remote, peer).start())
    backward(near)
    peers("near", lambda peer: d_copy(remote, peer).start())
    d_recv[me] = d_send[me]

    coef_rows = stacked(coefs)
    half_rows = half * chunk
    in_other = slope_ref.at[pl.ds(0, half_rows), pl.ds(0, feature)]
    in_mine = slope_ref.at[pl.ds(half_rows, half_rows), pl.ds(0, feature)]

    def weight_chunk(step, in_target, hidden_target, slot):
        span = pl.ds(pl.multiple_of(step * chunk, chunk), chunk)
        in_target[pl.ds(pl.multiple_of(slot * chunk, chunk), chunk), :] = mm(
            pre_ref[span, :], a_recv[...].reshape(rows_all, feature)
        )
        hidden = folded(nt(coef_rows, act_ref[span, :]))
        hidden_target[slot] = hidden
        return folded(mm(stacked(hidden), out_ref[span, :]))

    tower = jnp.zeros((8, feature), F32)
    tower = lax.fori_loop(
        0,
        half,
        lambda i, total: total + weight_chunk(other * half + i, in_other, hidden_other, i),
        tower,
    )
    in_copy = to_other(0, in_other, in_sum_ref)
    hidden_copy = to_other(1, hidden_other, hidden_recv)
    in_copy.start()
    hidden_copy.start()
    tower = lax.fori_loop(
        0,
        half,
        lambda i, total: total + weight_chunk(core * half + i, in_mine, hidden_mine, i),
        tower,
    )
    t_send[...] = tower[0:2]
    t_recv[me] = tower[0:2]
    everyone(lambda peer: t_copy(remote, peer).start())
    gate = 2.0 * folded(mm(coef_rows, a_recv[...].reshape(rows_all, feature)))

    tiles = stacked(b_recv[:, near].reshape(count * 8, 128))

    def at_home(key):
        found = look_up(tiles, key)
        return jnp.where(row_of == 0, found[0], found[1])

    first_dot, second_dot = at_home(first_key), at_home(second_key)
    task_logit = gate_first * first_dot + gate_second * second_dot + bias
    logit_grad = LOSS_SCALE * (sigmoid(task_logit) - labels)
    first_grad = logit_grad * (first_dot - second_dot) * gate_first * gate_second
    gate_input = jnp.zeros((tok_rows, feature), F32)
    for task in range(2):
        high, low = halves(signed * first_grad[task : task + 1, :])
        gate_input += mm(high.astype(BF16), gates[task], 0, 0)
        gate_input += mm(low.astype(BF16), gates[task], 0, 0)
    high, low = halves(gate_input)
    bag_acc[...] = mm(bag, high.astype(BF16)) + mm(bag, low.astype(BF16))

    everyone(lambda peer: a_copy(remote, peer).wait_send())
    everyone(lambda peer: m_copy(remote, peer).wait_send())
    for index in range(2):
        everyone(lambda peer, index=index: b_copy(remote, peer, index).wait_send())

    def bag_part(row_span, index):
        lane_span = pl.ds(pl.multiple_of(index * slots, 128), slots)
        back = d_recv[pl.ds(index * group, group)].reshape(slots, feature)
        return mm(bag_place_ref[row_span, lane_span], back)

    peers("near", lambda peer: d_copy(arrival, peer).wait_recv())
    bag_acc[...] += bag_part(pl.ds(0, entries), near)
    weight_lanes = jnp.broadcast_to(weight_col, (entries, 128))
    match_rows = entries // 2
    bag_weights[...] = weight_lanes
    peers("far", lambda peer: d_copy(arrival, peer).wait_recv())
    for which, index in (("far", far), ("near", near)):
        row_span = pl.ds(pl.multiple_of(index * match_rows, 8), match_rows)
        weights = jnp.concatenate([bag_weights[row_span, :]] * (feature // 128), axis=1)
        rows = weights * (bag_acc[row_span, :] + bag_part(row_span, far))
        e_send[pl.ds(index * group, group)] = rows.astype(BF16).reshape(group, held, feature)
        peers(which, lambda peer: e_copy(remote, peer).start())

    def forwarded(peer, source):
        return to_other(4 + peer, source, e_other.at[peer])

    e_recv[me] = e_send[me]
    forwarded(me, e_send.at[me]).start()

    hidden_copy.wait()
    tower_three = jnp.concatenate(
        [tower_high.astype(F32), tower_low.astype(F32), tower_high.astype(F32)], axis=0
    ).astype(BF16)

    @pl.loop(0, half)
    def _(step):
        span = pl.ds(pl.multiple_of(step * chunk, chunk), chunk)
        high, low = halves(hidden_mine[step] + hidden_recv[step])
        three = jnp.concatenate([high, high, low], axis=0).astype(BF16)
        out_sum_ref[span, :] = mm(three, tower_three, 0, 0)

    everyone(lambda peer: t_copy(arrival, peer).wait_recv())
    summed = t_recv[0]
    for source in range(1, count):
        summed = summed + t_recv[source]
    mine = jnp.concatenate([summed, gate[2:4], jnp.zeros((4, feature), F32)], axis=0)
    s_send[...] = mine
    small_copy = to_other(3, s_send, s_recv)
    small_copy.start()
    in_copy.wait()

    @pl.loop(0, half)
    def _(step):
        span = pl.ds(pl.multiple_of(step * chunk, chunk), chunk)
        in_sum_ref[span, :] = in_sum_ref[span, :] + in_mine[span, :]

    everyone(lambda peer: d_copy(remote, peer).wait_send())
    everyone(lambda peer: t_copy(remote, peer).wait_send())
    rows_copy.wait()
    loads[11].wait()
    table_rows = table_ref.shape[0]
    part = table_rows // 4
    sides = ((rows_mine, e_recv, pre_ref.at[pl.ds(0, table_rows), pl.ds(0, entries)]),)
    sides += ((rows_other, e_other, pre_ref.at[pl.ds(table_rows, table_rows), pl.ds(0, entries)]),)

    @pl.loop(0, 4)
    def _(step):
        span = pl.ds(pl.multiple_of(step * part, part), part)
        rows = (iota((part, entries), 0) + step * part).astype(F32)
        for rows_ref, _, match_ref in sides:
            match_ref[span, :] = one_hot(rows == rows_ref[0:1, :]).astype(BF16)

    def gather(side, index):
        _, source_ref, match_ref = side
        sources = source_ref[pl.ds(index * group, group)].reshape(group * held, feature)
        lane_span = pl.ds(pl.multiple_of(index * (entries // 2), 128), entries // 2)

        @pl.loop(0, 4)
        def _(step):
            span = pl.ds(pl.multiple_of(step * part, part), part)
            table_ref[span, :] = table_ref[span, :] - STEP_SIZE * mm(
                match_ref[span, lane_span], sources
            )

    def landed(peer):
        e_copy(arrival, peer).wait_recv()
        forwarded(peer, e_recv.at[peer]).start()

    def crossed(peer):
        forwarded(peer, e_recv.at[peer]).wait()

    peers("near", landed)
    gather(sides[0], near)
    peers("near", crossed)
    crossed(me)
    gather(sides[1], near)
    peers("far", landed)
    gather(sides[0], far)
    small_copy.wait()
    both = mine + s_recv[...]
    tower_sum_ref[...] = both[0:2]
    gate_sum_ref[...] = both[2:4]
    everyone(lambda peer: e_copy(remote, peer).wait_send())

    peers("far", crossed)
    gather(sides[1], far)


def write_out(*refs):
    sources, targets, sem = refs[:5], refs[5:10], refs[10]
    copies = []
    for source, target in zip(sources, targets, strict=True):
        parts = 4 if source.shape[0] % 32 == 0 else 1
        rows = source.shape[0] // parts
        for part in range(parts):
            span = pl.ds(part * rows, rows)
            copies.append(
                pltpu.make_async_copy(source.at[span], target.at[span], sem.at[len(copies)])
            )
            copies[-1].start()
    for copy in copies:
        copy.wait()


def on_device(
    pooled,
    routes,
    labels,
    in_weight,
    out_weight,
    gate_weight,
    tower_weight,
    tower_bias,
    bag_rows,
    bag_sample,
    bag_weight,
    row_table,
):
    count = lax.axis_size("expert")
    tok_rows, feature = pooled.shape
    tasks = tower_weight.shape[0]
    hidden = in_weight.shape[1]
    cap = -(-(3 * tok_rows // count) // 8) * 8
    rows_all = count * cap
    chunk = 1024 if rows_all * 1024 < 2**20 else 512
    chunks = hidden // chunk
    per_owner = bag_rows.shape[0] // count
    held = -(-per_owner // 8) * 8
    entries = count * held

    def bags(values, empty):
        if held == per_owner:
            return values
        return jnp.pad(
            values.reshape(count, per_owner), ((0, 0), (0, held - per_owner)), constant_values=empty
        )

    vmem = pl.BlockSpec(memory_space=pltpu.VMEM)
    anywhere = pl.BlockSpec(memory_space=pl.ANY)
    routed = (count, cap, feature)
    owned = (count, held, feature)
    half_rows = hidden // 2
    halved = (chunks // 2, 8, chunk)
    in_hbm = [
        pltpu.with_memory_space_constraint(value, pltpu.HBM)
        for value in (
            pooled,
            routes.T,
            labels.T,
            in_weight[0],
            out_weight[0],
            gate_weight,
            tower_weight,
            tower_bias,
            bag_rows.reshape(-1, 128),
            bags(bag_sample, -1).reshape(1, -1),
            bags(bag_weight, 0.0).reshape(1, -1),
            row_table,
        )
    ]
    results = pl.pallas_call(
        functools.partial(kernel, (count, cap, chunk, chunks, per_owner)),
        out_shape=(
            pltpu.VMEM((half_rows, feature), F32),
            pltpu.VMEM((half_rows, feature), F32),
            pltpu.VMEM((tasks, feature), F32),
            pltpu.VMEM((tasks, feature), F32),
            pltpu.VMEM(row_table.shape, F32),
        ),
        in_specs=[anywhere] * 12,
        out_specs=(vmem,) * 5,
        scratch_shapes=[
            pltpu.VMEM(pooled.shape, BF16),
            pltpu.VMEM((2, tok_rows), jnp.int32),
            pltpu.VMEM((2, tok_rows), jnp.int32),
            pltpu.VMEM(gate_weight.shape, BF16),
            pltpu.VMEM(tower_weight.shape, F32),
            pltpu.SMEM(tower_bias.shape, F32),
            pltpu.VMEM((bag_rows.shape[0] // 128, 128), jnp.int32),
            pltpu.VMEM((1, entries), jnp.int32),
            pltpu.VMEM((1, entries), F32),
            pltpu.VMEM((hidden, feature), BF16),
            pltpu.VMEM((hidden, feature), BF16),
            pltpu.VMEM((chunks, feature, chunk), BF16),
            pltpu.VMEM((chunks, 16, chunk), BF16),
            pltpu.VMEM((2, hidden, 128), F32),
            pltpu.VMEM((hidden, rows_all), BF16),
            pltpu.VMEM((hidden, rows_all), F32),
            pltpu.VMEM((hidden, rows_all), BF16),
            pltpu.VMEM((entries, rows_all), BF16),
            pltpu.VMEM((entries, feature), F32),
            pltpu.VMEM((entries, 128), F32),
            pltpu.VMEM(routed, BF16),
            pltpu.VMEM(routed, BF16),
            pltpu.VMEM((count, 2, 128), F32),
            pltpu.VMEM((count, 2, 128), F32),
            pltpu.VMEM((2, 8, 128), F32),
            pltpu.VMEM((count, 2, 8, 128), F32),
            pltpu.VMEM(routed, BF16),
            pltpu.VMEM(routed, BF16),
            pltpu.VMEM(owned, BF16),
            pltpu.VMEM(owned, BF16),
            pltpu.VMEM(owned, BF16),
            pltpu.VMEM((2, feature), F32),
            pltpu.VMEM((count, 2, feature), F32),
            pltpu.VMEM((8, feature), F32),
            pltpu.VMEM((8, feature), F32),
            pltpu.VMEM((8, entries), F32),
            pltpu.VMEM((8, entries), F32),
            pltpu.VMEM(halved, F32),
            pltpu.VMEM(halved, F32),
            pltpu.VMEM(halved, F32),
            pltpu.VMEM((16, rows_all), F32),
            pltpu.VMEM((feature, rows_all), F32),
            pltpu.SemaphoreType.DMA((7, count)),
            pltpu.SemaphoreType.DMA((7, count)),
            pltpu.SemaphoreType.DMA((4 + count,)),
            pltpu.SemaphoreType.DMA((4 + count,)),
            pltpu.SemaphoreType.DMA((12,)),
        ],
        compiler_params=pltpu.CompilerParams(
            collective_id=0, has_side_effects=True, vmem_limit_bytes=VMEM_LIMIT
        ),
    )(*in_hbm)
    in_grad, out_grad, gate_grad, tower_grad, table = pl.pallas_call(
        write_out,
        out_shape=[jax.ShapeDtypeStruct(value.shape, F32) for value in results],
        in_specs=[vmem] * 5,
        out_specs=[anywhere] * 5,
        scratch_shapes=[pltpu.SemaphoreType.DMA((20,))],
        compiler_params=pltpu.CompilerParams(vmem_limit_bytes=2**20),
    )(*[pltpu.with_memory_space_constraint(value, pltpu.VMEM) for value in results])
    return (in_grad[None], out_grad[None], gate_grad[None], tower_grad, table)


def solution(mesh):
    in_specs = (
        P(("expert", "dp"), None),
        P(("expert", "dp"), None),
        P(("expert", "dp"), None),
        P("expert", None, None),
        P("expert", None, None),
        P(),
        P(),
        P(),
        P(("expert", "dp")),
        P(("expert", "dp")),
        P(("expert", "dp")),
        P("expert", None),
    )
    out_specs = (
        P("expert", "dp", None),
        P("expert", "dp", None),
        P("expert", None, None),
        P(),
        P("expert", None),
    )
    return jax.shard_map(
        on_device, mesh=mesh, in_specs=in_specs, out_specs=out_specs, check_vma=False
    )
```

time: 76.1 us -> 52.2 us (0.69)
  Pallas kernels: 66.2 us -> 51.4 us
  other arithmetic: 5.53 us -> 0 us
  matrix products: 1.81 us -> 0 us
  local copies, waits for them, and re-layouts: 1.64 us -> 0 us
    pallas_call x1, Pallas kernels: 66.2 us -> 48.9 us  [on_device(): pl.pallas_call(functools.partial(kernel, (count, cap, chunk, chunks, per_...]
    broadcast_in_dim x1 -> x0, other arithmetic: 3.85 us -> none  [on_device(): in_grad = (in_mine + in_other)[None]]
    pallas_call x0 -> x1, Pallas kernels: none -> 2.51 us  [on_device(): pl.pallas_call(write_out, out_shape=[jax.ShapeDtypeStruct(value.shape, F3...]
    dot_general x1 -> x0, matrix products: 1.81 us -> none  [mm(): lax.dot_general(left, right, (((left_dim,), (right_dim,)), ((), ())), pre...]
    add x2 -> x0, other arithmetic: 1.69 us -> none  [the longest x1 1.68 us: on_device(): sum((hidden_sum[:, t].reshape(-1, 1) * tower_weight[t][None, :] for t in...]
    slice x4 -> x0, local copies, waits for them, and re-layouts: 1.55 us -> none  [the longest x1 0.95 us: on_device(): owned_rows = rows[:, :, 0, :held].reshape(-1)]
where the time goes in v1:
time: 52.2 us; the launch traced here: 52 us
  Pallas kernels  51.4 us (98%)
  between operations  0.64 us (1%)
    pallas_call x1, Pallas kernels, on_device(): pl.pallas_call(functools.partial(kernel, (count, cap, chunk, chunks, per_...  48.9 us
    pallas_call x1, Pallas kernels, on_device(): pl.pallas_call(write_out, out_shape=[jax.ShapeDtypeStruct(value.shape, F3...  2.51 us

profile of v1, /device:TPU:0, one launch (start us, length us, event | category | flops | bytes accessed | tf_op | source)
XLA Modules:
  0.0 52.0 jit_solution(1679589653800843754)
XLA Ops:
  0.6 48.9 %shard_map.155 = (f32[2048,256]{1,0:T(8,128)S(1)}, f32[2048,256]{1,0:T(8,128)S(1)}, f32[2,256]{1,0:T(2,128)S(1)}, f32[2,256]{1,0:T(2,128)S(1)}, f32[1024,256]{1,0:T(8,128)S(1)}) custom-call(bf16[256,256]{1,0:T(8,128)(2,1)} %pooled_hbm.1, s32[2,256]{1,0:T(2,128)} %bitcast.12, s32[2,256]{1,0:T(2,128)} %bitcast.13, bf16[4096,256]{1,0:T(8,128)(2,1)} %bitcast.10, ...), custom_call_target="tpu_custom_call" | custom-call | tf_op jit(solution)/shard_map/pallas_call | solution.py:714
  49.5 2.5 %shard_map.156 = (f32[2048,256]{1,0:T(8,128)}, f32[2048,256]{1,0:T(8,128)}, f32[2,256]{1,0:T(2,128)}, f32[2,256]{1,0:T(2,128)}, f32[1024,256]{1,0:T(8,128)}) custom-call(f32[2048,256]{1,0:T(8,128)S(1)} %get-tuple-element.15.refs_0_, f32[2048,256]{1,0:T(8,128)S(1)} %get-tuple-element.16.refs_1_, f32[2,256]{1,0:T(2,128)S(1)} %get-tuple-element.17.refs_2_, ...), custom_call_target="tpu_custom_call" | custom-call | tf_op jit(solution)/shard_map/pallas_call | solution.py:778

commit v2 on v1

--- a/solution.py
+++ b/solution.py
@@ -11,7 +11,7 @@
 STEP_SIZE = 0.25
 F32, BF16 = jnp.float32, jnp.bfloat16
 MESH = pl.DeviceIdType.MESH
-VMEM_LIMIT = 56 * 2**20
+VMEM_LIMIT = 47 * 2**20
 SLOT_BASE = 4096
 
 
@@ -83,6 +83,9 @@
     out_sum_ref,
     gate_sum_ref,
     tower_sum_ref,
+    e_recv,
+    e_other,
+    pre_ref,
     table_ref,
     pooled_ref,
     routes_rows_ref,
@@ -100,7 +103,6 @@
     proj_cols_ref,
     act_ref,
     slope_ref,
-    pre_ref,
     bag_place_ref,
     bag_acc,
     bag_weights,
@@ -113,8 +115,6 @@
     d_send,
     d_recv,
     e_send,
-    e_recv,
-    e_other,
     t_send,
     t_recv,
     s_send,
@@ -147,42 +147,38 @@
     held = e_send.shape[1]
     entries = count * held
 
-    def remote(phase, peer, source, target):
+    def copy(phase, peer, sent, source, target, slot):
         return pltpu.make_async_remote_copy(
             src_ref=source,
             dst_ref=target,
-            send_sem=send_sem.at[phase, peer],
-            recv_sem=recv_sem.at[phase, me],
+            send_sem=send_sem.at[phase, sent],
+            recv_sem=recv_sem.at[phase, slot],
             device_id={"expert": peer},
             device_id_type=MESH,
         )
 
-    def arrival(phase, peer, source, target):
-        return pltpu.make_async_remote_copy(
-            src_ref=source,
-            dst_ref=target,
-            send_sem=send_sem.at[phase, peer],
-            recv_sem=recv_sem.at[phase, peer],
-            device_id={"expert": peer},
-            device_id_type=MESH,
-        )
-
-    def peers(which, act):
-        if which == "far":
-
-            @pl.loop(0, group)
-            def _(step):
-                act(far * group + lax.rem(place_in + step, group))
-
-        else:
-
-            @pl.loop(1, group)
-            def _(step):
-                act(near * group + lax.rem(place_in + step, group))
-
-    def everyone(act):
-        peers("far", act)
-        peers("near", act)
+    def onward(which, act):
+        @pl.loop(1 if which == "near" else 0, group)
+        def _(step):
+            start = (near if which == "near" else far) * group
+            act(start + lax.rem(place_in + step, group), near * group + step)
+
+    def backward_from(which, low, high, act):
+        @pl.loop(max(low, 1) if which == "near" else low, high)
+        def _(position):
+            start = (near if which == "near" else far) * group
+            act(start + lax.rem(place_in - position + group, group), start + position)
+
+    def everyone_on(act):
+        onward("far", act)
+        onward("near", act)
+
+    def everyone_back(act):
+        backward_from("near", 0, group, act)
+        backward_from("far", 0, group, act)
+
+    def rows_at(slot, size):
+        return pl.ds(pl.multiple_of(slot * size, 8), size)
 
     def to_other(index, source, target):
         return pltpu.make_async_remote_copy(
@@ -194,23 +190,24 @@
             device_id_type=MESH,
         )
 
-    def a_copy(make, peer):
-        return make(0, peer, a_send.at[peer], a_recv.at[me if make is remote else peer])
-
-    def m_copy(make, peer):
-        return make(1, peer, m_send.at[peer], m_recv.at[me if make is remote else peer])
-
-    def b_copy(make, peer, index):
-        return make(2 + index, peer, b_send.at[index], b_recv.at[me if make is remote else peer, index])
-
-    def d_copy(make, peer):
-        return make(4, peer, d_send.at[peer], d_recv.at[me if make is remote else peer])
-
-    def e_copy(make, peer):
-        return make(5, peer, e_send.at[peer], e_recv.at[me if make is remote else peer])
-
-    def t_copy(make, peer):
-        return make(6, peer, t_send, t_recv.at[me if make is remote else peer])
+    def a_copy(peer, slot):
+        return copy(0, peer, peer, a_send.at[rows_at(peer, cap)], a_recv.at[rows_at(slot, cap)], slot)
+
+    def m_copy(peer, slot):
+        return copy(1, peer, peer, m_send.at[peer], m_recv.at[slot], slot)
+
+    def b_copy(peer, slot, index):
+        return copy(2 + index, peer, peer, b_send.at[index], b_recv.at[slot, index], slot)
+
+    def d_copy(peer, position, slot):
+        source = d_send.at[rows_at(position, cap)]
+        return copy(4, peer, position, source, d_recv.at[rows_at(slot, cap)], slot)
+
+    def e_copy(peer, slot):
+        return copy(5, peer, peer, e_send.at[peer], e_recv.at[slot], slot)
+
+    def t_copy(peer, slot):
+        return copy(6, peer, peer, t_send, t_recv.at[slot], slot)
 
     barrier = pltpu.get_barrier_semaphore()
 
@@ -265,15 +262,18 @@
 
     def send_half(index):
         rows = 0.5 * mm(fill_of(index), pooled_ref[...])
-        a_send[pl.ds(index * group, group)] = rows.astype(BF16).reshape(group, cap, feature)
+        a_send[rows_at(index, slots), :] = rows.astype(BF16)
+
+    def far_start():
+        onward("far", lambda peer, slot: a_copy(peer, slot).start())
 
     loads[1].wait()
     send_half(near)
     pl.semaphore_wait(barrier, count)
-    peers("near", lambda peer: a_copy(remote, peer).start())
+    onward("near", lambda peer, slot: a_copy(peer, slot).start())
     send_half(far)
-    peers("far", lambda peer: a_copy(remote, peer).start())
-    a_recv[me] = a_send[me]
+    pl.when(core == 1)(far_start)
+    a_recv[rows_at(near * group, cap), :] = a_send[rows_at(me, cap), :]
     for load in loads[2:5]:
         load.wait()
 
@@ -289,10 +289,13 @@
     told = nt(partner(first_map, second_row, second_rank), first_at) + nt(
         partner(second_map, first_row, first_rank), second_at
     )
+    def position_at(expert):
+        ahead = jnp.where(expert >= group, expert - group, expert) - place_in
+        return jnp.where(ahead < 0, ahead + group, ahead)
+
     code = told[count:]
-    meta = jnp.where(
-        code > 0.0, SLOT_BASE * told[:count] + code + (4 * cap * place_in).astype(F32), 0.0
-    )
+    ahead = (4 * cap * position_at(told[:count].astype(jnp.int32))).astype(F32)
+    meta = jnp.where(code > 0.0, SLOT_BASE * told[:count] + code + ahead, 0.0)
     piece_lane = iota((1, 128), 1)
     for owner in range(count):
         start = owner * per_owner
@@ -301,8 +304,7 @@
             line = pltpu.roll(jnp.broadcast_to(line, (8, 128)), 128 - start % 128, 1)[0:1, :]
         m_send[owner, 0:1, :] = meta[owner : owner + 1, :]
         m_send[owner, 1:2, :] = jnp.where(piece_lane < per_owner, line, -1.0)
-    everyone(lambda peer: m_copy(remote, peer).start())
-    m_recv[me] = m_send[me]
+    m_recv[near * group] = m_send[me]
 
     feat_row = iota((8, feature), 0)
     tower_rows = jnp.where(
@@ -313,8 +315,9 @@
     for load in loads[5:11]:
         load.wait()
 
-    @pl.loop(0, chunks)
-    def _(step):
+    early = chunks // 2
+
+    def project(step):
         span = pl.ds(pl.multiple_of(step * chunk, chunk), chunk)
         weights = out_ref[span, :]
         proj_rows_ref[step] = stacked(nt(tower_high, weights) + nt(tower_low, weights))
@@ -323,25 +326,34 @@
         proj_cols_ref[1, span, :] = jnp.broadcast_to(cols[:, 1:2], (chunk, 128))
         turned_ref[step] = in_ref[span, :].T
 
+    pl.loop(0, early)(project)
+    pl.when(core == 0)(far_start)
+    pl.loop(early, chunks)(project)
     rows_acc[...] = jnp.zeros_like(rows_acc)
     back_acc[...] = jnp.zeros_like(back_acc)
 
-    def forward(index):
-        lane_span = pl.ds(pl.multiple_of(index * slots, 128), slots)
-        features = a_recv.at[pl.ds(index * group, group)]
-
-        @pl.loop(0, chunks)
-        def _(step):
-            span = pl.ds(pl.multiple_of(step * chunk, chunk), chunk)
-            close = nt(in_ref[span, :], features[...].reshape(slots, feature))
-            bend = jnp.tanh(close)
-            bent = close * bend
-            slope_ref[span, lane_span] = (1.0 + bend) + (close - bent * bend)
-            act = (close + bent).astype(BF16)
-            act_ref[span, lane_span] = act
-            rows_acc[:, lane_span] += mm(proj_rows_ref[step], act)
-
-        dots = folded(rows_acc[:, lane_span])
+    def lanes_of(index, low, width):
+        return pl.ds(pl.multiple_of(index * slots + low, 128), width)
+
+    def forward(index, low, width, per):
+        lane_span = lanes_of(index, low, width)
+
+        @pl.loop(0, chunks // per)
+        def _(outer):
+            for inner in range(per):
+                step = outer * per + inner
+                span = pl.ds(pl.multiple_of(step * chunk, chunk), chunk)
+                close = nt(in_ref[span, :], a_recv[lane_span, :])
+                bend = jnp.tanh(close)
+                twice = 1.0 + bend
+                full = close * twice
+                slope_ref[span, lane_span] = twice + full * (1.0 - bend)
+                act = full.astype(BF16)
+                act_ref[span, lane_span] = act
+                rows_acc[:, lane_span] += mm(proj_rows_ref[step], act)
+
+    def tell(index):
+        dots = folded(rows_acc[:, lanes_of(index, 0, slots)])
         tile_row = iota((8, 128), 0)
         tile = jnp.zeros((8, 128), F32)
         for task in range(2):
@@ -350,14 +362,20 @@
                 tile = jnp.where(tile_row == task * blocks + block, piece, tile)
         b_send[index] = tile
         b_recv[me, index] = tile
-        everyone(lambda peer: b_copy(remote, peer, index).start())
-
-    peers("near", lambda peer: a_copy(arrival, peer).wait_recv())
-    forward(near)
-    peers("far", lambda peer: a_copy(arrival, peer).wait_recv())
-    forward(far)
-
-    everyone(lambda peer: m_copy(arrival, peer).wait_recv())
+        everyone_on(lambda peer, slot: b_copy(peer, me, index).start())
+
+    def a_wait(which, low, high):
+        backward_from(which, low, high, lambda peer, slot: a_copy(peer, slot).wait_recv())
+
+    a_wait("near", 0, group)
+    forward(near, 0, slots, 1)
+    a_wait("far", 0, group)
+    everyone_on(lambda peer, slot: m_copy(peer, slot).start())
+    tell(near)
+    forward(far, 0, slots, 1)
+    tell(far)
+
+    everyone_back(lambda peer, slot: m_copy(peer, slot).wait_recv())
     pieces = [m_recv[source] for source in range(count)]
     told = jnp.concatenate(
         [lane_pack(pieces[i * group : (i + 1) * group], cap, slots)[0:1, :] for i in range(2)],
@@ -401,7 +419,7 @@
     gates = [gate_ref[:, task, :] for task in range(2)]
     expert_row = iota((count, rows_all), 0)
     sign = one_hot(expert_row == me) - one_hot(expert_row == pair_expert)
-    features_all = a_recv[...].reshape(rows_all, feature)
+    features_all = a_recv[...]
     slot_gate = jnp.zeros((8, rows_all), F32)
     for task in range(2):
         logits = nt(gates[task], features_all)
@@ -425,8 +443,8 @@
         )
     gate_first = sigmoid(gate_logit)
     gate_second = 1.0 - gate_first
-    first_key = dot_key(first_row, first_rank + cap * place_in)
-    second_key = dot_key(second_row, second_rank + cap * place_in)
+    first_key = dot_key(first_row, first_rank + cap * position_at(first_row))
+    second_key = dot_key(second_row, second_rank + cap * position_at(second_row))
     sample_wide = jnp.broadcast_to(bag_sample_ref[...].astype(F32), (8, entries))
     weight_wide = jnp.broadcast_to(bag_weight_ref[...], (8, entries))
     sample_col, weight_col = sample_wide.T[:, 0:1], weight_wide.T[:, 0:1]
@@ -435,7 +453,7 @@
         bag_place_ref[:, index * slots : (index + 1) * slots] = nt(bag, fill_of(index)).astype(BF16)
 
     for index in range(2):
-        everyone(lambda peer, index=index: b_copy(arrival, peer, index).wait_recv())
+        everyone_back(lambda peer, slot, index=index: b_copy(peer, peer, index).wait_recv())
 
     own_dot = folded(rows_acc[...])
     pair_dot = []
@@ -453,65 +471,34 @@
     )
     rows_acc[0:8, :] = coefs
 
-    def backward(index):
-        lane_span = pl.ds(pl.multiple_of(index * slots, 128), slots)
+    def backward(index, low, width, per):
+        lane_span = lanes_of(index, low, width)
         coef_zero, coef_one = rows_acc[0:1, lane_span], rows_acc[1:2, lane_span]
 
-        @pl.loop(0, chunks)
-        def _(step):
-            span = pl.ds(pl.multiple_of(step * chunk, chunk), chunk)
-            zero, one = (
-                jnp.concatenate([proj_cols_ref[task, span, :]] * blocks, axis=1) for task in range(2)
-            )
-            hidden_grad = zero * coef_zero + one * coef_one
-            grad = (hidden_grad * slope_ref[span, lane_span]).astype(BF16)
-            pre_ref[span, lane_span] = grad
-            back_acc[:, lane_span] += mm(turned_ref[step], grad)
-
-        back = 0.5 * back_acc[:, lane_span].T
-        d_send[pl.ds(index * group, group)] = back.astype(BF16).reshape(group, cap, feature)
-
-    backward(far)
-    peers("far", lambda peer: d_copy(remote, peer).start())
-    backward(near)
-    peers("near", lambda peer: d_copy(remote, peer).start())
-    d_recv[me] = d_send[me]
-
-    coef_rows = stacked(coefs)
-    half_rows = half * chunk
-    in_other = slope_ref.at[pl.ds(0, half_rows), pl.ds(0, feature)]
-    in_mine = slope_ref.at[pl.ds(half_rows, half_rows), pl.ds(0, feature)]
-
-    def weight_chunk(step, in_target, hidden_target, slot):
-        span = pl.ds(pl.multiple_of(step * chunk, chunk), chunk)
-        in_target[pl.ds(pl.multiple_of(slot * chunk, chunk), chunk), :] = mm(
-            pre_ref[span, :], a_recv[...].reshape(rows_all, feature)
-        )
-        hidden = folded(nt(coef_rows, act_ref[span, :]))
-        hidden_target[slot] = hidden
-        return folded(mm(stacked(hidden), out_ref[span, :]))
-
-    tower = jnp.zeros((8, feature), F32)
-    tower = lax.fori_loop(
-        0,
-        half,
-        lambda i, total: total + weight_chunk(other * half + i, in_other, hidden_other, i),
-        tower,
-    )
-    in_copy = to_other(0, in_other, in_sum_ref)
-    hidden_copy = to_other(1, hidden_other, hidden_recv)
-    in_copy.start()
-    hidden_copy.start()
-    tower = lax.fori_loop(
-        0,
-        half,
-        lambda i, total: total + weight_chunk(core * half + i, in_mine, hidden_mine, i),
-        tower,
-    )
-    t_send[...] = tower[0:2]
-    t_recv[me] = tower[0:2]
-    everyone(lambda peer: t_copy(remote, peer).start())
-    gate = 2.0 * folded(mm(coef_rows, a_recv[...].reshape(rows_all, feature)))
+        @pl.loop(0, chunks // per)
+        def _(outer):
+            for inner in range(per):
+                step = outer * per + inner
+                span = pl.ds(pl.multiple_of(step * chunk, chunk), chunk)
+                zero, one = (
+                    jnp.concatenate([proj_cols_ref[task, span, :]] * (width // 128), axis=1)
+                    for task in range(2)
+                )
+                hidden_grad = zero * coef_zero + one * coef_one
+                grad = (hidden_grad * slope_ref[span, lane_span]).astype(BF16)
+                pre_ref[span, lane_span] = grad
+                back_acc[:, lane_span] += mm(turned_ref[step], grad)
+
+        d_send[lane_span, :] = (0.5 * back_acc[:, lane_span].T).astype(BF16)
+
+    def d_start(which, low, high):
+        backward_from(which, low, high, lambda peer, slot: d_copy(peer, slot, me).start())
+
+    backward(far, 0, slots, 1)
+    d_start("far", 0, group)
+    backward(near, 0, slots, 1)
+    d_start("near", 0, group)
+    d_recv[rows_at(me, cap), :] = d_send[rows_at(near * group, cap), :]
 
     tiles = stacked(b_recv[:, near].reshape(count * 8, 128))
 
@@ -530,35 +517,72 @@
         gate_input += mm(low.astype(BF16), gates[task], 0, 0)
     high, low = halves(gate_input)
     bag_acc[...] = mm(bag, high.astype(BF16)) + mm(bag, low.astype(BF16))
-
-    everyone(lambda peer: a_copy(remote, peer).wait_send())
-    everyone(lambda peer: m_copy(remote, peer).wait_send())
+    bag_weights[...] = jnp.broadcast_to(weight_col, (entries, 128))
+
+    coef_rows = stacked(coefs)
+    half_rows = half * chunk
+    in_other = slope_ref.at[pl.ds(0, half_rows), pl.ds(0, feature)]
+    in_mine = slope_ref.at[pl.ds(half_rows, half_rows), pl.ds(0, feature)]
+
+    def hidden_chunk(step, target, slot):
+        span = pl.ds(pl.multiple_of(step * chunk, chunk), chunk)
+        hidden = folded(nt(coef_rows, act_ref[span, :]))
+        target[slot] = hidden
+        return folded(mm(stacked(hidden), out_ref[span, :]))
+
+    def in_chunks(start, target):
+        @pl.loop(0, half)
+        def _(slot):
+            span = pl.ds(pl.multiple_of((start + slot) * chunk, chunk), chunk)
+            target[pl.ds(pl.multiple_of(slot * chunk, chunk), chunk), :] = mm(
+                pre_ref[span, :], a_recv[...]
+            )
+
+    in_chunks(other * half, in_other)
+    in_copy = to_other(0, in_other, in_sum_ref)
+    in_copy.start()
+    tower = jnp.zeros((8, feature), F32)
+    for target, start in ((hidden_other, other * half), (hidden_mine, core * half)):
+        tower = lax.fori_loop(
+            0, half, lambda i, total, target=target, start=start: total + hidden_chunk(start + i, target, i), tower
+        )
+    hidden_copy = to_other(1, hidden_other, hidden_recv)
+    hidden_copy.start()
+    t_send[...] = tower[0:2]
+    t_recv[me] = tower[0:2]
+
+    everyone_on(lambda peer, slot: a_copy(peer, slot).wait_send())
+    everyone_on(lambda peer, slot: m_copy(peer, slot).wait_send())
     for index in range(2):
-        everyone(lambda peer, index=index: b_copy(remote, peer, index).wait_send())
+        everyone_on(lambda peer, slot, index=index: b_copy(peer, me, index).wait_send())
 
     def bag_part(row_span, index):
         lane_span = pl.ds(pl.multiple_of(index * slots, 128), slots)
-        back = d_recv[pl.ds(index * group, group)].reshape(slots, feature)
-        return mm(bag_place_ref[row_span, lane_span], back)
-
-    peers("near", lambda peer: d_copy(arrival, peer).wait_recv())
+        return mm(bag_place_ref[row_span, lane_span], d_recv[rows_at(index, slots), :])
+
+    def d_wait(which):
+        backward_from(which, 0, group, lambda peer, slot: d_copy(peer, slot, peer).wait_recv())
+
+    d_wait("near")
     bag_acc[...] += bag_part(pl.ds(0, entries), near)
-    weight_lanes = jnp.broadcast_to(weight_col, (entries, 128))
     match_rows = entries // 2
-    bag_weights[...] = weight_lanes
-    peers("far", lambda peer: d_copy(arrival, peer).wait_recv())
+    d_wait("far")
+    everyone_on(lambda peer, slot: t_copy(peer, me).start())
     for which, index in (("far", far), ("near", near)):
         row_span = pl.ds(pl.multiple_of(index * match_rows, 8), match_rows)
         weights = jnp.concatenate([bag_weights[row_span, :]] * (feature // 128), axis=1)
         rows = weights * (bag_acc[row_span, :] + bag_part(row_span, far))
         e_send[pl.ds(index * group, group)] = rows.astype(BF16).reshape(group, held, feature)
-        peers(which, lambda peer: e_copy(remote, peer).start())
-
-    def forwarded(peer, source):
-        return to_other(4 + peer, source, e_other.at[peer])
-
-    e_recv[me] = e_send[me]
-    forwarded(me, e_send.at[me]).start()
+        onward(which, lambda peer, slot: e_copy(peer, slot).start())
+
+    def forwarded(slot, source):
+        return to_other(4 + slot, source, e_other.at[slot])
+
+    e_recv[near * group] = e_send[me]
+    forwarded(near * group, e_send.at[me]).start()
+
+    in_chunks(core * half, in_mine)
+    gate = 2.0 * folded(mm(coef_rows, a_recv[...]))
 
     hidden_copy.wait()
     tower_three = jnp.concatenate(
@@ -572,7 +596,42 @@
         three = jnp.concatenate([high, high, low], axis=0).astype(BF16)
         out_sum_ref[span, :] = mm(three, tower_three, 0, 0)
 
-    everyone(lambda peer: t_copy(arrival, peer).wait_recv())
+    in_copy.wait()
+
+    @pl.loop(0, half)
+    def _(step):
+        span = pl.ds(pl.multiple_of(step * chunk, chunk), chunk)
+        in_sum_ref[span, :] = in_sum_ref[span, :] + in_mine[span, :]
+
+    for which in ("far", "near"):
+        backward_from(which, 0, group, lambda peer, slot: d_copy(peer, slot, me).wait_send())
+    rows_copy.wait()
+    loads[11].wait()
+    table_rows = table_ref.shape[0]
+    part = table_rows // 4
+
+    @pl.loop(0, 4)
+    def _(step):
+        numbers = (iota((part, entries), 0) + step * part).astype(F32)
+        for index, row_numbers in enumerate((rows_mine, rows_other)):
+            span = pl.ds(pl.multiple_of(index * table_rows + step * part, part), part)
+            pre_ref[span, pl.ds(0, entries)] = jnp.where(
+                numbers == row_numbers[0:1, :], STEP_SIZE, 0.0
+            ).astype(BF16)
+
+    def landed(peer, slot):
+        e_copy(peer, slot).wait_recv()
+        forwarded(slot, e_recv.at[slot]).start()
+
+    def gather(index, values):
+        half_entries = entries // 2
+        lane_span = pl.ds(pl.multiple_of(near * half_entries, 128), half_entries)
+        match = pre_ref[pl.ds(index * table_rows, table_rows), lane_span]
+        sources = values[pl.ds(near * group, group)].reshape(half_entries, feature)
+        table_ref[...] = table_ref[...] - mm(match, sources)
+
+    backward_from("near", 0, group, landed)
+    everyone_back(lambda peer, slot: t_copy(peer, peer).wait_recv())
     summed = t_recv[0]
     for source in range(1, count):
         summed = summed + t_recv[source]
@@ -580,77 +639,69 @@
     s_send[...] = mine
     small_copy = to_other(3, s_send, s_recv)
     small_copy.start()
-    in_copy.wait()
-
-    @pl.loop(0, half)
-    def _(step):
-        span = pl.ds(pl.multiple_of(step * chunk, chunk), chunk)
-        in_sum_ref[span, :] = in_sum_ref[span, :] + in_mine[span, :]
-
-    everyone(lambda peer: d_copy(remote, peer).wait_send())
-    everyone(lambda peer: t_copy(remote, peer).wait_send())
-    rows_copy.wait()
-    loads[11].wait()
-    table_rows = table_ref.shape[0]
-    part = table_rows // 4
-    sides = ((rows_mine, e_recv, pre_ref.at[pl.ds(0, table_rows), pl.ds(0, entries)]),)
-    sides += ((rows_other, e_other, pre_ref.at[pl.ds(table_rows, table_rows), pl.ds(0, entries)]),)
-
-    @pl.loop(0, 4)
-    def _(step):
-        span = pl.ds(pl.multiple_of(step * part, part), part)
-        rows = (iota((part, entries), 0) + step * part).astype(F32)
-        for rows_ref, _, match_ref in sides:
-            match_ref[span, :] = one_hot(rows == rows_ref[0:1, :]).astype(BF16)
-
-    def gather(side, index):
-        _, source_ref, match_ref = side
-        sources = source_ref[pl.ds(index * group, group)].reshape(group * held, feature)
-        lane_span = pl.ds(pl.multiple_of(index * (entries // 2), 128), entries // 2)
-
-        @pl.loop(0, 4)
-        def _(step):
-            span = pl.ds(pl.multiple_of(step * part, part), part)
-            table_ref[span, :] = table_ref[span, :] - STEP_SIZE * mm(
-                match_ref[span, lane_span], sources
-            )
-
-    def landed(peer):
-        e_copy(arrival, peer).wait_recv()
-        forwarded(peer, e_recv.at[peer]).start()
-
-    def crossed(peer):
-        forwarded(peer, e_recv.at[peer]).wait()
-
-    peers("near", landed)
-    gather(sides[0], near)
-    peers("near", crossed)
-    crossed(me)
-    gather(sides[1], near)
-    peers("far", landed)
-    gather(sides[0], far)
+    everyone_on(lambda peer, slot: t_copy(peer, me).wait_send())
+    gather(0, e_recv)
+    backward_from("far", 0, group, landed)
+    everyone_on(lambda peer, slot: e_copy(peer, slot).wait_send())
     small_copy.wait()
     both = mine + s_recv[...]
     tower_sum_ref[...] = both[0:2]
     gate_sum_ref[...] = both[2:4]
-    everyone(lambda peer: e_copy(remote, peer).wait_send())
-
-    peers("far", crossed)
-    gather(sides[1], far)
-
-
-def write_out(*refs):
-    sources, targets, sem = refs[:5], refs[5:10], refs[10]
+
+    def crossed(peer, slot):
+        forwarded(slot, e_recv.at[slot]).wait()
+
+    crossed(me, near * group)
+    backward_from("near", 0, group, crossed)
+    gather(1, e_other)
+    backward_from("far", 0, group, crossed)
+
+
+def write_out(
+    in_sum,
+    out_sum,
+    gate_sum,
+    tower_sum,
+    e_recv,
+    e_other,
+    matches,
+    table_ref,
+    in_out,
+    out_out,
+    gate_out,
+    tower_out,
+    table_out,
+    sem,
+):
     copies = []
-    for source, target in zip(sources, targets, strict=True):
-        parts = 4 if source.shape[0] % 32 == 0 else 1
-        rows = source.shape[0] // parts
-        for part in range(parts):
+
+    def start(source, target):
+        copies.append(pltpu.make_async_copy(source, target, sem.at[len(copies)]))
+        copies[-1].start()
+
+    for source, target in ((in_sum, in_out), (out_sum, out_out)):
+        rows = source.shape[0] // 4
+        for part in range(4):
             span = pl.ds(part * rows, rows)
-            copies.append(
-                pltpu.make_async_copy(source.at[span], target.at[span], sem.at[len(copies)])
-            )
-            copies[-1].start()
+            start(source.at[span], target.at[span])
+    start(gate_sum, gate_out)
+    start(tower_sum, tower_out)
+    group, held = e_recv.shape[0] // 2, e_recv.shape[1]
+    half = group * held
+    far = 1 - lax.div(lax.axis_index("expert"), group)
+    lane_span = pl.ds(pl.multiple_of(far * half, 128), half)
+    far_values = [
+        values[pl.ds(far * group, group)].reshape(half, values.shape[2]) for values in (e_recv, e_other)
+    ]
+    table_rows = table_ref.shape[0]
+    rows = table_rows // 4
+    for part in range(4):
+        span = pl.ds(part * rows, rows)
+        total = table_ref[span, :]
+        for index, values in enumerate(far_values):
+            total = total - mm(matches[pl.ds(index * table_rows + part * rows, rows), lane_span], values)
+        table_ref[span, :] = total
+        start(table_ref.at[span], table_out.at[span])
     for copy in copies:
         copy.wait()
 
@@ -690,7 +741,7 @@
 
     vmem = pl.BlockSpec(memory_space=pltpu.VMEM)
     anywhere = pl.BlockSpec(memory_space=pl.ANY)
-    routed = (count, cap, feature)
+    routed = (rows_all, feature)
     owned = (count, held, feature)
     half_rows = hidden // 2
     halved = (chunks // 2, 8, chunk)
@@ -718,10 +769,13 @@
             pltpu.VMEM((half_rows, feature), F32),
             pltpu.VMEM((tasks, feature), F32),
             pltpu.VMEM((tasks, feature), F32),
+            pltpu.VMEM(owned, BF16),
+            pltpu.VMEM(owned, BF16),
+            pltpu.VMEM((hidden, rows_all), BF16),
             pltpu.VMEM(row_table.shape, F32),
         ),
         in_specs=[anywhere] * 12,
-        out_specs=(vmem,) * 5,
+        out_specs=(vmem,) * 8,
         scratch_shapes=[
             pltpu.VMEM(pooled.shape, BF16),
             pltpu.VMEM((2, tok_rows), jnp.int32),
@@ -739,7 +793,6 @@
             pltpu.VMEM((2, hidden, 128), F32),
             pltpu.VMEM((hidden, rows_all), BF16),
             pltpu.VMEM((hidden, rows_all), F32),
-            pltpu.VMEM((hidden, rows_all), BF16),
             pltpu.VMEM((entries, rows_all), BF16),
             pltpu.VMEM((entries, feature), F32),
             pltpu.VMEM((entries, 128), F32),
@@ -751,8 +804,6 @@
             pltpu.VMEM((count, 2, 8, 128), F32),
             pltpu.VMEM(routed, BF16),
             pltpu.VMEM(routed, BF16),
-            pltpu.VMEM(owned, BF16),
-            pltpu.VMEM(owned, BF16),
             pltpu.VMEM(owned, BF16),
             pltpu.VMEM((2, feature), F32),
             pltpu.VMEM((count, 2, feature), F32),
@@ -777,11 +828,12 @@
     )(*in_hbm)
     in_grad, out_grad, gate_grad, tower_grad, table = pl.pallas_call(
         write_out,
-        out_shape=[jax.ShapeDtypeStruct(value.shape, F32) for value in results],
-        in_specs=[vmem] * 5,
+        out_shape=[jax.ShapeDtypeStruct(value.shape, F32) for value in results[:4]]
+        + [jax.ShapeDtypeStruct(row_table.shape, F32)],
+        in_specs=[vmem] * 8,
         out_specs=[anywhere] * 5,
-        scratch_shapes=[pltpu.SemaphoreType.DMA((20,))],
-        compiler_params=pltpu.CompilerParams(vmem_limit_bytes=2**20),
+        scratch_shapes=[pltpu.SemaphoreType.DMA((16,))],
+        compiler_params=pltpu.CompilerParams(vmem_limit_bytes=4 * 2**20),
     )(*[pltpu.with_memory_space_constraint(value, pltpu.VMEM) for value in results])
     return (in_grad[None], out_grad[None], gate_grad[None], tower_grad, table)
 

time: 52.2 us -> 50.7 us (0.971)
  Pallas kernels: 51.4 us -> 49.9 us
    pallas_call x1, Pallas kernels: 48.9 us -> 47.4 us  [on_device(): pl.pallas_call(functools.partial(kernel, (count, cap, chunk, chunks, per_...]
where the time goes in v2:
time: 50.7 us; the launch traced here: 50.5 us
  Pallas kernels  49.9 us (98%)
  between operations  0.64 us (1%)
    pallas_call x1, Pallas kernels, on_device(): pl.pallas_call(functools.partial(kernel, (count, cap, chunk, chunks, per_...  47.4 us
    pallas_call x1, Pallas kernels, on_device(): pl.pallas_call(write_out, out_shape=[jax.ShapeDtypeStruct(value.shape, F3...  2.49 us

profile of v2, /device:TPU:0, one launch (start us, length us, event | category | flops | bytes accessed | tf_op | source)
XLA Modules:
  0.0 50.5 jit_solution(15218737769487610776)
XLA Ops:
  0.6 47.4 %shard_map.155 = (f32[2048,256]{1,0:T(8,128)S(1)}, f32[2048,256]{1,0:T(8,128)S(1)}, f32[2,256]{1,0:T(2,128)S(1)}, f32[2,256]{1,0:T(2,128)S(1)}, bf16[16,32,256]{...) custom-call(bf16[256,256]{1,0:T(8,128)(2,1)} %pooled_hbm.1, ...), custom_call_target="tpu_custom_call" | custom-call | tf_op jit(solution)/shard_map/pallas_call | solution.py:765
  48.0 2.5 %shard_map.156 = (f32[2048,256]{1,0:T(8,128)}, f32[2048,256]{1,0:T(8,128)}, f32[2,256]{1,0:T(2,128)}, f32[2,256]{1,0:T(2,128)}, f32[1024,256]{1,0:T(8,128)}) custom-call(f32[2048,256]{1,0:T(8,128)S(1)} %get-tuple-element.18.in_sum, f32[2048,256]{1,0:T(8,128)S(1)} %get-tuple-element.19.out_sum, f32[2,256]{1,0:T(2,128)S(1)} %get-tuple-element.20.gate_sum, ...), custom_call_target="tpu_custom_call" | custom-call | tf_op jit(solution)/shard_map/pallas_call | solution.py:829

commit v3 on v2

--- a/solution.py
+++ b/solution.py
@@ -311,19 +311,25 @@
         feat_row == 0, tower_ref[0:1, :], jnp.where(feat_row == 1, tower_ref[1:2, :], 0.0)
     )
     tower_high, tower_low = halves(tower_rows)
+    tower_two = stacked(tower_rows)
+    wide_rows = iota((256, feature), 0) < 128
+    wide_high, wide_low = (
+        jnp.where(wide_rows, part[0:1, :], part[1:2, :]).astype(BF16)
+        for part in (tower_high, tower_low)
+    )
     tower_high, tower_low = tower_high.astype(BF16), tower_low.astype(BF16)
     for load in loads[5:11]:
         load.wait()
 
-    early = chunks // 2
+    early = chunks // 4
 
     def project(step):
         span = pl.ds(pl.multiple_of(step * chunk, chunk), chunk)
         weights = out_ref[span, :]
-        proj_rows_ref[step] = stacked(nt(tower_high, weights) + nt(tower_low, weights))
-        cols = nt(weights, tower_high) + nt(weights, tower_low)
-        proj_cols_ref[0, span, :] = jnp.broadcast_to(cols[:, 0:1], (chunk, 128))
-        proj_cols_ref[1, span, :] = jnp.broadcast_to(cols[:, 1:2], (chunk, 128))
+        proj_rows_ref[step] = stacked(folded(nt(tower_two, weights)))
+        wide = nt(weights, wide_high) + nt(weights, wide_low)
+        proj_cols_ref[0, span, :] = wide[:, :128]
+        proj_cols_ref[1, span, :] = wide[:, 128:]
         turned_ref[step] = in_ref[span, :].T
 
     pl.loop(0, early)(project)
@@ -368,11 +374,11 @@
         backward_from(which, low, high, lambda peer, slot: a_copy(peer, slot).wait_recv())
 
     a_wait("near", 0, group)
-    forward(near, 0, slots, 1)
+    forward(near, 0, slots, 2)
     a_wait("far", 0, group)
     everyone_on(lambda peer, slot: m_copy(peer, slot).start())
     tell(near)
-    forward(far, 0, slots, 1)
+    forward(far, 0, slots, 2)
     tell(far)
 
     everyone_back(lambda peer, slot: m_copy(peer, slot).wait_recv())
@@ -494,9 +500,9 @@
     def d_start(which, low, high):
         backward_from(which, low, high, lambda peer, slot: d_copy(peer, slot, me).start())
 
-    backward(far, 0, slots, 1)
+    backward(far, 0, slots, 2)
     d_start("far", 0, group)
-    backward(near, 0, slots, 1)
+    backward(near, 0, slots, 2)
     d_start("near", 0, group)
     d_recv[rows_at(me, cap), :] = d_send[rows_at(near * group, cap), :]
 

time: 50.7 us -> 49.4 us (0.974)
  Pallas kernels: 49.9 us -> 48.6 us
    pallas_call x1, Pallas kernels: 47.4 us -> 46.1 us  [on_device(): pl.pallas_call(functools.partial(kernel, (count, cap, chunk, chunks, per_...]
where the time goes in v3:
time: 49.4 us; the launch traced here: 49.3 us
  Pallas kernels  48.6 us (98%)
  between operations  0.64 us (1%)
    pallas_call x1, Pallas kernels, on_device(): pl.pallas_call(functools.partial(kernel, (count, cap, chunk, chunks, per_...  46.1 us
    pallas_call x1, Pallas kernels, on_device(): pl.pallas_call(write_out, out_shape=[jax.ShapeDtypeStruct(value.shape, F3...  2.49 us

profile of v3, /device:TPU:0, one launch (start us, length us, event | category | flops | bytes accessed | tf_op | source)
XLA Modules:
  0.0 49.3 jit_solution(1517371436821598033)
XLA Ops:
  0.6 46.1 %shard_map.155 = (f32[2048,256]{1,0:T(8,128)S(1)}, f32[2048,256]{1,0:T(8,128)S(1)}, f32[2,256]{1,0:T(2,128)S(1)}, f32[2,256]{1,0:T(2,128)S(1)}, bf16[16,32,256]{...) custom-call(bf16[256,256]{1,0:T(8,128)(2,1)} %pooled_hbm.1, ...), custom_call_target="tpu_custom_call" | custom-call | tf_op jit(solution)/shard_map/pallas_call | solution.py:771
  46.8 2.5 %shard_map.156 = (f32[2048,256]{1,0:T(8,128)}, f32[2048,256]{1,0:T(8,128)}, f32[2,256]{1,0:T(2,128)}, f32[2,256]{1,0:T(2,128)}, f32[1024,256]{1,0:T(8,128)}) custom-call(f32[2048,256]{1,0:T(8,128)S(1)} %get-tuple-element.18.in_sum, f32[2048,256]{1,0:T(8,128)S(1)} %get-tuple-element.19.out_sum, f32[2,256]{1,0:T(2,128)S(1)} %get-tuple-element.20.gate_sum, ...), custom_call_target="tpu_custom_call" | custom-call | tf_op jit(solution)/shard_map/pallas_call | solution.py:835

commit v4 on v3

--- a/solution.py
+++ b/solution.py
@@ -557,10 +557,13 @@
     t_send[...] = tower[0:2]
     t_recv[me] = tower[0:2]
 
-    everyone_on(lambda peer, slot: a_copy(peer, slot).wait_send())
-    everyone_on(lambda peer, slot: m_copy(peer, slot).wait_send())
-    for index in range(2):
-        everyone_on(lambda peer, slot, index=index: b_copy(peer, me, index).wait_send())
+    def drain():
+        everyone_on(lambda peer, slot: a_copy(peer, slot).wait_send())
+        everyone_on(lambda peer, slot: m_copy(peer, slot).wait_send())
+        for index in range(2):
+            everyone_on(lambda peer, slot, index=index: b_copy(peer, me, index).wait_send())
+
+    pl.when(core == 1)(drain)
 
     def bag_part(row_span, index):
         lane_span = pl.ds(pl.multiple_of(index * slots, 128), slots)
@@ -590,6 +593,7 @@
     in_chunks(core * half, in_mine)
     gate = 2.0 * folded(mm(coef_rows, a_recv[...]))
 
+    pl.when(core == 0)(drain)
     hidden_copy.wait()
     tower_three = jnp.concatenate(
         [tower_high.astype(F32), tower_low.astype(F32), tower_high.astype(F32)], axis=0

time: 49.4 us -> 49.1 us (level)
  no operation moved by 1% of the time
where the time goes in v4:
time: 49.1 us; the launch traced here: 48.9 us
  Pallas kernels  48.3 us (98%)
  between operations  0.64 us (1%)
    pallas_call x1, Pallas kernels, on_device(): pl.pallas_call(functools.partial(kernel, (count, cap, chunk, chunks, per_...  45.8 us
    pallas_call x1, Pallas kernels, on_device(): pl.pallas_call(write_out, out_shape=[jax.ShapeDtypeStruct(value.shape, F3...  2.49 us

profile of v4, /device:TPU:0, one launch (start us, length us, event | category | flops | bytes accessed | tf_op | source)
XLA Modules:
  0.0 48.9 jit_solution(11338331003750423901)
XLA Ops:
  0.6 45.8 %shard_map.155 = (f32[2048,256]{1,0:T(8,128)S(1)}, f32[2048,256]{1,0:T(8,128)S(1)}, f32[2,256]{1,0:T(2,128)S(1)}, f32[2,256]{1,0:T(2,128)S(1)}, bf16[16,32,256]{...) custom-call(bf16[256,256]{1,0:T(8,128)(2,1)} %pooled_hbm.1, ...), custom_call_target="tpu_custom_call" | custom-call | tf_op jit(solution)/shard_map/pallas_call | solution.py:775
  46.4 2.5 %shard_map.156 = (f32[2048,256]{1,0:T(8,128)}, f32[2048,256]{1,0:T(8,128)}, f32[2,256]{1,0:T(2,128)}, f32[2,256]{1,0:T(2,128)}, f32[1024,256]{1,0:T(8,128)}) custom-call(f32[2048,256]{1,0:T(8,128)S(1)} %get-tuple-element.18.in_sum, f32[2048,256]{1,0:T(8,128)S(1)} %get-tuple-element.19.out_sum, f32[2,256]{1,0:T(2,128)S(1)} %get-tuple-element.20.gate_sum, ...), custom_call_target="tpu_custom_call" | custom-call | tf_op jit(solution)/shard_map/pallas_call | solution.py:839
